TPU v7x, 256 devices: a whole 4x4x8 slice. The times are simulated.
256 devices in a mesh: expert: 4 (over x_lo, core), node: 64 (over y, z, x_hi).
Axes of the slice: x: 4 (x_hi: 2, x_lo: 2; x = x_hi * 2 + x_lo), y: 4, z: 8, core: 2. Of those that a mesh axis runs over, the one named last changes fastest.
Arguments:
- tokens: bfloat16 [2, 65536, 1024], P(None, ('expert', 'node')), may hold values from -6 to 6
- routing: int32 [2, 65536], P(None, ('expert', 'node')), may hold values from 0 to 3, as said below
- out_grad: bfloat16 [2, 65536, 512], P(None, ('expert', 'node')), may hold values from -6 to 6
- weights: float32 [64, 4, 1024, 512], P('node', 'expert'), may hold values from -5 to 5
- momentum: float32 [64, 4, 1024, 512], P('node', 'expert'), may hold values from -8 to 8
Outputs:
- new_weights: float32 [64, 4, 1024, 512], P('node', 'expert')
- new_momentum: float32 [64, 4, 1024, 512], P('node', 'expert')
- in_grad: bfloat16 [2, 65536, 1024], P(None, ('expert', 'node'))
Inputs may be any that keep to these rules, and one draw needn't show every extreme that they name: `routing`: within each block of 256 rows of one round (the rows of one device), no expert is named more than 128 times; in every round each node has one expert that is named exactly 128 times in each of that node's blocks.
All inputs are finite; a program needn't handle non-finite values.
Results may differ from a plain program's by a relative error of at most 0.0065.
Values may be sent and summed in bfloat16 or wider, within the bound.
A program may use at most 64 MiB of HBM per device.

v0:
```python
import math

import jax
import jax.numpy as jnp
from jax import lax
from jax.sharding import PartitionSpec as P

ROUNDS = 2
NS_STEPS = 3


def shifted(block, axis, distance):
    devices = range(lax.axis_size(axis))
    route = [((i - distance) % len(devices), i) for i in devices]
    return lax.ppermute(block, axis, route)


def dispatch_table(route, experts_all, capacity):
    labels = jnp.arange(experts_all, dtype=jnp.int32)
    onehot = (route[:, None] == labels[None, :]).astype(jnp.int32)
    slot_rank = jnp.sum(onehot * (jnp.cumsum(onehot, axis=0) - 1), axis=1)
    target = route * capacity + slot_rank
    slot_ids = jnp.arange(experts_all * capacity, dtype=jnp.int32)
    return (slot_ids[:, None] == target[None, :]).astype(jnp.bfloat16)


def orthogonalize(moment):
    frob_norm = jnp.sqrt(jnp.sum(moment * moment))
    orthog = (moment / (frob_norm + 1e-07)).astype(jnp.bfloat16)
    for sweep in range(NS_STEPS):
        gram_matrix = lax.dot_general(
            orthog, orthog, (((0,), (0,)), ((), ())), preferred_element_type=jnp.float32
        ).astype(jnp.bfloat16)
        square = jnp.dot(gram_matrix, gram_matrix, preferred_element_type=jnp.float32)
        polynom = (-4.775 * gram_matrix.astype(jnp.float32) + 2.0315 * square).astype(jnp.bfloat16)
        orthog = (
            3.4445 * orthog.astype(jnp.float32)
            + jnp.dot(orthog, polynom, preferred_element_type=jnp.float32)
        ).astype(jnp.bfloat16)
    return orthog


def on_device(tokens, routing, out_grad, weights, momentum):
    row_count = tokens.shape[1]
    model_width = tokens.shape[2]
    hidden_width = out_grad.shape[2]
    capacity = row_count // 2
    experts_all = weights.shape[1] * lax.axis_size("expert")
    factor = 1.0 / math.sqrt(model_width)
    step_size = 0.1 * math.sqrt(model_width)
    weight = weights[0, 0]
    moment = momentum[0, 0]
    tables = []
    sent_rows = []
    sent_grads = []
    for round_index in range(ROUNDS):
        dispatch = dispatch_table(routing[round_index], experts_all, capacity)
        tables.append(dispatch)
        sent_rows.append(
            jnp.dot(dispatch, tokens[round_index], preferred_element_type=jnp.float32)
            .astype(jnp.bfloat16)
            .reshape(experts_all, capacity, model_width)
        )
        sent_grads.append(
            jnp.dot(dispatch, out_grad[round_index], preferred_element_type=jnp.float32)
            .astype(jnp.bfloat16)
            .reshape(experts_all, capacity, hidden_width)
        )
    in_grads = []
    for round_index in range(ROUNDS):
        got_rows, got_grads = (
            lax.all_to_all(
                sent_rows[round_index], "expert", split_axis=0, concat_axis=0, tiled=True
            ),
            lax.all_to_all(
                sent_grads[round_index], "expert", split_axis=0, concat_axis=0, tiled=True
            ),
        )
        got_rows = got_rows.reshape(-1, model_width)
        got_grads = got_grads.reshape(-1, hidden_width)
        shaped = weight.astype(jnp.bfloat16)
        preact = jnp.dot(got_rows, shaped, preferred_element_type=jnp.float32) * factor
        slopes = (got_grads.astype(jnp.float32) * 2.0 * jnp.maximum(preact, 0.0)).astype(
            jnp.bfloat16
        )
        backward = (
            lax.dot_general(
                slopes, shaped, (((1,), (1,)), ((), ())), preferred_element_type=jnp.float32
            )
            * factor
        )
        backward = backward.astype(jnp.bfloat16).reshape(-1, capacity, model_width)
        grad_w = (
            lax.dot_general(
                got_rows, slopes, (((0,), (0,)), ((), ())), preferred_element_type=jnp.float32
            )
            * factor
        )
        returned = lax.all_to_all(
            backward, "expert", split_axis=0, concat_axis=0, tiled=True
        ).reshape(-1, model_width)
        in_grads.append(
            lax.dot_general(
                tables[round_index],
                returned,
                (((0,), (0,)), ((), ())),
                preferred_element_type=jnp.float32,
            ).astype(jnp.bfloat16)
        )
        moment = 0.9 * moment + grad_w
        orthog = orthogonalize(moment)
        stepped = weight - step_size * orthog.astype(jnp.float32)
        shared = stepped.astype(jnp.bfloat16)
        near_left = shifted(shared, "node", 1)
        near_right = shifted(shared, "node", -1)
        far_left = shifted(shared, "node", 2)
        far_right = shifted(shared, "node", -2)
        neighbours = near_left.astype(jnp.float32) + near_right.astype(jnp.float32)
        neighbours = neighbours + far_left.astype(jnp.float32) + far_right.astype(jnp.float32)
        weight = 0.4 * stepped + 0.15 * neighbours
    return (weight[None, None], moment[None, None], jnp.stack(in_grads))


def solution(mesh):
    return jax.shard_map(
        on_device,
        mesh=mesh,
        in_specs=(
            P(None, ("expert", "node"), None),
            P(None, ("expert", "node")),
            P(None, ("expert", "node"), None),
            P("node", "expert", None, None),
            P("node", "expert", None, None),
        ),
        out_specs=(
            P("node", "expert", None, None),
            P("node", "expert", None, None),
            P(None, ("expert", "node"), None),
        ),
        check_vma=False,
    )
```

profile of v0, /device:TPU:1, one launch (start us, length us, event | category | flops | bytes accessed | tf_op | source)
XLA Modules:
  0.0 253.1 jit_solution(8718090989142973463)
XLA Ops:
  0.6 0.0 copy-start.11
  0.6 0.8 fusion.79
  1.4 1.2 reduce-window.14
  2.7 0.1 slice.40
  2.7 0.1 copy.8
  2.9 0.1 copy.9
  3.0 0.1 add_bitcast_fusion.2
  3.1 1.2 reduce-window.16
  4.3 0.1 slice.41
  4.3 0.1 copy.10
  4.5 0.1 copy.11
  4.6 0.1 add_bitcast_fusion.1
  4.7 0.8 multiply_add_fusion.2
  5.5 2.1 convolution_convert_fusion.5
  7.5 6.7 %all-to-all-start.1 = ((bf16[4,128,512]{2,1,0:T(8,128)(2,1)}), bf16[4,128,512]{2,1,0:T(8,128)(2,1)S(1)}, u32[]{:S(2)}, u32[]{:S(2)}) async-start(bf16[4,128,512]{2,1,0:T(8,128)(2,1)} %bitcast.12), calls=%async_computation.1 | async-start | bytes 1048576 | tf_op jit(solution)/shard_map/all_to_all | solution.py:75
  14.2 1.4 convolution_convert_fusion.1
  15.6 6.6 %all-to-all-done.1 = bf16[4,128,512]{2,1,0:T(8,128)(2,1)S(1)} async-done(((bf16[4,128,512]{2,1,0:T(8,128)(2,1)}), bf16[4,128,512]{2,1,0:T(8,128)(2,1)S(1)}, u32[]{:S(2)}, u32[]{:S(2)}) %all-to-all-start.1) | async-done | bytes 524320 | tf_op jit(solution)/shard_map/all_to_all | solution.py:75
  22.2 0.8 copy-done.8
  23.0 4.4 %all-to-all-start = ((bf16[4,128,1024]{2,1,0:T(8,128)(2,1)}), bf16[4,128,1024]{2,1,0:T(8,128)(2,1)S(1)}, u32[]{:S(2)}, u32[]{:S(2)}) async-start(bf16[4,128,1024]{2,1,0:T(8,128)(2,1)} %bitcast.128), calls=%async_computation | async-start | bytes 2097152 | tf_op jit(solution)/shard_map/all_to_all | solution.py:72
  27.3 2.2 convert_multiply_fusion.1
  29.5 11.4 %all-to-all-done = bf16[4,128,1024]{2,1,0:T(8,128)(2,1)S(1)} async-done(((bf16[4,128,1024]{2,1,0:T(8,128)(2,1)}), bf16[4,128,1024]{2,1,0:T(8,128)(2,1)S(1)}, u32[]{:S(2)}, u32[]{:S(2)}) %all-to-all-start) | async-done | bytes 1048608 | tf_op jit(solution)/shard_map/all_to_all | solution.py:72
  40.9 2.1 fusion.17
  43.1 2.7 %multiply_reduce_fusion.1 = (f32[]{:T(128)}, f32[1024,512]{1,0:T(8,128)}) fusion(bf16[512,1024]{1,0:T(8,128)(2,1)S(1)} %bitcast.124, bf16[512,512]{1,0:T(8,128)(2,1)S(1)} %fusion.17, f32[1,1,1024,512]{3,2,1,0:T(8,128)S(1)} %copy-done.7), kind=kOutput, calls=%fused_computation.18 | convolution fusion | flops 539492352 | bytes 5767172 | tf_op jit(solution)/shard_map/dot_general | solution.py:94
  46.4 3.8 %convolution_convert_fusion.11 = bf16[512,512]{1,0:T(8,128)(2,1)} fusion(f32[1024,512]{1,0:T(8,128)} %get-tuple-element.8, f32[]{:T(128)S(6)} %add.88), kind=kOutput, calls=%fused_computation.56 | convolution fusion | flops 538181632 | bytes 2621444 | tf_op jit(solution)/shard_map/dot_general | solution.py:31
  50.2 4.1 %add_convert_fusion.5 = bf16[1024,512]{1,0:T(8,128)(2,1)S(1)} fusion(bf16[512,512]{1,0:T(8,128)(2,1)} %convolution_convert_fusion.11, f32[1024,512]{1,0:T(8,128)} %get-tuple-element.8, f32[]{:T(128)S(6)} %add.88), kind=kOutput, calls=%fused_computation.16 | convolution fusion | flops 810811392 | bytes 3670020 | tf_op jit(solution)/shard_map/dot_general | solution.py:38
  54.3 1.5 convolution_convert_fusion.10
  55.9 3.5 %add_convert_fusion.4 = bf16[1024,512]{1,0:T(8,128)(2,1)} fusion(bf16[1024,512]{1,0:T(8,128)(2,1)S(1)} %add_convert_fusion.5, bf16[512,512]{1,0:T(8,128)(2,1)} %convolution_convert_fusion.10), kind=kOutput, calls=%fused_computation.15 | convolution fusion | flops 808714240 | bytes 2621440 | tf_op jit(solution)/shard_map/dot_general | solution.py:38
  59.4 2.3 convolution_convert_fusion.9
  61.7 4.4 %fusion.80 = (bf16[1024,512]{1,0:T(8,128)(2,1)}, f32[1024,512]{1,0:T(8,128)}) fusion(bf16[1024,512]{1,0:T(8,128)(2,1)} %add_convert_fusion.4, bf16[512,512]{1,0:T(8,128)(2,1)S(1)} %convolution_convert_fusion.9, f32[1,1,1024,512]{3,2,1,0:T(8,128)S(1)} %copy-done), kind=kOutput, calls=%fused_computation.133 | convolution fusion | flops 810811392 | bytes 6815744 | tf_op jit(solution)/shard_map/dot_general | solution.py:38
  66.1 1.0 collective-permute-start
  67.1 7.7 %collective-permute-start.1 = (bf16[1024,512]{1,0:T(8,128)(2,1)}, bf16[1024,512]{1,0:T(8,128)(2,1)}, u32[]{:S(2)}, u32[]{:S(2)}) collective-permute-start(bf16[1024,512]{1,0:T(8,128)(2,1)} %get-tuple-element.9), channel_id=1, source_target_pairs={{1,0},{2,1},{3,2},{4,3},{5,4},{6,5},{7,6},{8,7},{9,8},{10,9},{11,1... | collective-permute-start | bytes 3145736 | tf_op jit(solution)/shard_map/ppermute | solution.py:15
  74.8 4.8 %collective-permute-start.3 = (bf16[1024,512]{1,0:T(8,128)(2,1)}, bf16[1024,512]{1,0:T(8,128)(2,1)}, u32[]{:S(2)}, u32[]{:S(2)}) collective-permute-start(bf16[1024,512]{1,0:T(8,128)(2,1)} %get-tuple-element.9), channel_id=1, source_target_pairs={{2,0},{3,1},{4,2},{5,3},{6,4},{7,5},{8,6},{9,7},{10,8},{11,9},{12,... | collective-permute-start | bytes 3145736 | tf_op jit(solution)/shard_map/ppermute | solution.py:15
  79.6 1.1 convolution_convert_fusion.4
  80.8 5.2 %all-to-all-start.3 = ((bf16[4,128,512]{2,1,0:T(8,128)(2,1)}), bf16[4,128,512]{2,1,0:T(8,128)(2,1)S(1)}, u32[]{:S(2)}, u32[]{:S(2)}) async-start(bf16[4,128,512]{2,1,0:T(8,128)(2,1)} %bitcast.25), calls=%async_computation.3 | async-start | bytes 1048576 | tf_op jit(solution)/shard_map/all_to_all | solution.py:75
  85.9 2.5 convolution_convert_fusion
  88.4 29.5 %all-to-all-done.3 = bf16[4,128,512]{2,1,0:T(8,128)(2,1)S(1)} async-done(((bf16[4,128,512]{2,1,0:T(8,128)(2,1)}), bf16[4,128,512]{2,1,0:T(8,128)(2,1)S(1)}, u32[]{:S(2)}, u32[]{:S(2)}) %all-to-all-start.3) | async-done | bytes 524320 | tf_op jit(solution)/shard_map/all_to_all | solution.py:75
  117.9 0.8 copy-done.9
  118.7 4.9 %all-to-all-start.2 = ((bf16[4,128,1024]{2,1,0:T(8,128)(2,1)}), bf16[4,128,1024]{2,1,0:T(8,128)(2,1)S(1)}, u32[]{:S(2)}, u32[]{:S(2)}) async-start(bf16[4,128,1024]{2,1,0:T(8,128)(2,1)} %bitcast.127), calls=%async_computation.2 | async-start | bytes 2097152 | tf_op jit(solution)/shard_map/all_to_all | solution.py:72
  123.5 2.2 convert_multiply_fusion
  125.7 2.9 %multiply_convert_fusion.1 = bf16[512,1024]{1,0:T(8,128)(2,1)} fusion(bf16[512,512]{1,0:T(8,128)(2,1)} %copy-done.4, f32[1,1,1024,512]{3,2,1,0:T(8,128)S(1)} %copy-done), kind=kOutput, calls=%fused_computation.4 | convolution fusion | flops 537919488 | bytes 3670016 | tf_op jit(solution)/shard_map/dot_general | solution.py:87
  128.7 6.0 %collective-permute-done.3 = bf16[1024,512]{1,0:T(8,128)(2,1)} collective-permute-done((bf16[1024,512]{1,0:T(8,128)(2,1)}, bf16[1024,512]{1,0:T(8,128)(2,1)}, u32[]{:S(2)}, u32[]{:S(2)}) %collective-permute-start.3) | collective-permute-done | bytes 1048608 | tf_op jit(solution)/shard_map/ppermute | solution.py:15
  134.7 2.9 %multiply_add_fusion.1 = f32[1024,512]{1,0:T(8,128)S(1)} fusion(bf16[1024,512]{1,0:T(8,128)(2,1)} %collective-permute-done.3, bf16[1024,512]{1,0:T(8,128)(2,1)} %collective-permute-done.2, bf16[1024,512]{1,0:T(8,128)(2,1)} %collective-permute-done.1, bf16[1024,512]{1,0:T(8,128)(2,1)} %collective-permute-done, f32[1024,512]{1,0:T(8,128)S(1)} %copy-done.2), kind=kLoop, calls=%fused_computation.13 | loop fusion | flops 5242880 | bytes 8388608 | tf_op jit(solution)/shard_map/add | solution.py:120
  137.6 6.0 %all-to-all-start.4 = ((bf16[4,128,1024]{2,1,0:T(8,128)(2,1)}), bf16[4,128,1024]{2,1,0:T(8,128)(2,1)}, u32[]{:S(2)}, u32[]{:S(2)}) async-start(bf16[4,128,1024]{2,1,0:T(8,128)(2,1)} %bitcast.125), calls=%async_computation.4 | async-start | bytes 2097152 | tf_op jit(solution)/shard_map/all_to_all | solution.py:99
  143.6 2.1 fusion.16
  145.7 2.7 %multiply_reduce_fusion = (f32[]{:T(128)}, f32[1024,512]{1,0:T(8,128)}) fusion(bf16[512,1024]{1,0:T(8,128)(2,1)S(1)} %bitcast.122, bf16[512,512]{1,0:T(8,128)(2,1)S(1)} %fusion.16, f32[1024,512]{1,0:T(8,128)S(1)} %copy-done.1), kind=kOutput, calls=%fused_computation.11 | convolution fusion | flops 539492352 | bytes 5767172 | tf_op jit(solution)/shard_map/dot_general | solution.py:94
  149.1 3.8 %convolution_convert_fusion.8 = bf16[512,512]{1,0:T(8,128)(2,1)} fusion(f32[1024,512]{1,0:T(8,128)} %get-tuple-element.12, f32[]{:T(128)S(6)} %add.101), kind=kOutput, calls=%fused_computation.53 | convolution fusion | flops 538181632 | bytes 2621444 | tf_op jit(solution)/shard_map/dot_general | solution.py:31
  152.8 3.8 %add_convert_fusion.2 = bf16[1024,512]{1,0:T(8,128)(2,1)S(1)} fusion(bf16[512,512]{1,0:T(8,128)(2,1)} %convolution_convert_fusion.8, f32[1024,512]{1,0:T(8,128)} %get-tuple-element.12, f32[]{:T(128)S(6)} %add.101), kind=kOutput, calls=%fused_computation.9 | convolution fusion | flops 810811392 | bytes 3670020 | tf_op jit(solution)/shard_map/dot_general | solution.py:38
  156.6 1.0 copy-done.13
  157.6 1.5 convolution_convert_fusion.7
  159.1 3.3 %add_convert_fusion.1 = bf16[1024,512]{1,0:T(8,128)(2,1)S(1)} fusion(bf16[1024,512]{1,0:T(8,128)(2,1)} %copy-done.13, bf16[512,512]{1,0:T(8,128)(2,1)} %convolution_convert_fusion.7), kind=kOutput, calls=%fused_computation.8 | convolution fusion | flops 808714240 | bytes 2621440 | tf_op jit(solution)/shard_map/dot_general | solution.py:38
  162.5 1.5 convolution_convert_fusion.6
  164.0 1.7 multiply_convert_fusion
  165.7 3.6 %all-to-all-start.5 = ((bf16[4,128,1024]{2,1,0:T(8,128)(2,1)}), bf16[4,128,1024]{2,1,0:T(8,128)(2,1)S(1)}, u32[]{:S(2)}, u32[]{:S(2)}) async-start(bf16[4,128,1024]{2,1,0:T(8,128)(2,1)} %bitcast.32), calls=%async_computation.5 | async-start | bytes 2097152 | tf_op jit(solution)/shard_map/all_to_all | solution.py:99
  169.3 4.9 %fusion.81 = (bf16[1024,512]{1,0:T(8,128)(2,1)}, f32[1024,512]{1,0:T(8,128)}) fusion(f32[1024,512]{1,0:T(8,128)S(1)} %multiply_add_fusion.1, bf16[1024,512]{1,0:T(8,128)(2,1)} %copy-done.10, bf16[512,512]{1,0:T(8,128)(2,1)} %convolution_convert_fusion.6), kind=kOutput, calls=%fused_computation.134 | convolution fusion | flops 810811392 | bytes 6815744 | tf_op jit(solution)/shard_map/dot_general | solution.py:38
  174.2 19.0 %collective-permute-start.4 = (bf16[1024,512]{1,0:T(8,128)(2,1)}, bf16[1024,512]{1,0:T(8,128)(2,1)}, u32[]{:S(2)}, u32[]{:S(2)}) collective-permute-start(bf16[1024,512]{1,0:T(8,128)(2,1)} %get-tuple-element.13), channel_id=1, source_target_pairs={{63,0},{0,1},{1,2},{2,3},{3,4},{4,5},{5,6},{6,7},{7,8},{8,9},{9,10... | collective-permute-start | bytes 3145736 | tf_op jit(solution)/shard_map/ppermute | solution.py:15
  193.3 1.2 collective-permute-start.6
  194.4 9.7 %collective-permute-start.7 = (bf16[1024,512]{1,0:T(8,128)(2,1)}, bf16[1024,512]{1,0:T(8,128)(2,1)}, u32[]{:S(2)}, u32[]{:S(2)}) collective-permute-start(bf16[1024,512]{1,0:T(8,128)(2,1)} %get-tuple-element.13), channel_id=1, source_target_pairs={{2,0},{3,1},{4,2},{5,3},{6,4},{7,5},{8,6},{9,7},{10,8},{11,9},{12,... | collective-permute-start | bytes 3145736 | tf_op jit(solution)/shard_map/ppermute | solution.py:15
  204.1 2.5 fusion.18
  206.6 0.5 fusion.19
  207.1 2.2 pad_maximum_fusion
  209.4 29.2 %collective-permute-done.4 = bf16[1024,512]{1,0:T(8,128)(2,1)} collective-permute-done((bf16[1024,512]{1,0:T(8,128)(2,1)}, bf16[1024,512]{1,0:T(8,128)(2,1)}, u32[]{:S(2)}, u32[]{:S(2)}) %collective-permute-start.4) | collective-permute-done | bytes 1048608 | tf_op jit(solution)/shard_map/ppermute | solution.py:15
  238.6 0.1 collective-permute-done.5
  238.7 10.2 %collective-permute-done.7 = bf16[1024,512]{1,0:T(8,128)(2,1)} collective-permute-done((bf16[1024,512]{1,0:T(8,128)(2,1)}, bf16[1024,512]{1,0:T(8,128)(2,1)}, u32[]{:S(2)}, u32[]{:S(2)}) %collective-permute-start.7) | collective-permute-done | bytes 1048608 | tf_op jit(solution)/shard_map/ppermute | solution.py:15
  248.9 4.2 %add_bitcast_fusion = f32[1,1,1024,512]{3,2,1,0:T(8,128)} fusion(bf16[1024,512]{1,0:T(8,128)(2,1)} %collective-permute-done.7, bf16[1024,512]{1,0:T(8,128)(2,1)} %collective-permute-done.6, bf16[1024,512]{1,0:T(8,128)(2,1)} %collective-permute-done.5, bf16[1024,512]{1,0:T(8,128)(2,1)} %collective-permute-done.4, f32[1024,512]{1,0:T(8,128)S(1)} %copy-done.3), kind=kLoop, calls=%fused_computation.5 | loop fusion | flops 5242880 | bytes 8388608 | tf_op jit(solution)/shard_map/broadcast_in_dim | solution.py:121
  (41 shorter events, 0.2 us)
Async XLA Ops:
  0.6 13.6 %copy-start.11 = (bf16[2,256,1024]{2,1,0:T(8,128)(2,1)S(1)}, bf16[2,256,1024]{2,1,0:T(8,128)(2,1)}, u32[]{:S(2)}) copy-start(bf16[2,256,1024]{2,1,0:T(8,128)(2,1)} %param.5) | copy-start | bytes 3145732
  7.5 14.7 %all-to-all-start.1 = ((bf16[4,128,512]{2,1,0:T(8,128)(2,1)}), bf16[4,128,512]{2,1,0:T(8,128)(2,1)S(1)}, u32[]{:S(2)}, u32[]{:S(2)}) async-start(bf16[4,128,512]{2,1,0:T(8,128)(2,1)} %bitcast.12), calls=%async_computation.1 | async-start | bytes 1048576 | tf_op jit(solution)/shard_map/all_to_all | solution.py:75
  15.6 25.3 %copy-start = (f32[1,1,1024,512]{3,2,1,0:T(8,128)S(1)}, f32[1,1,1024,512]{3,2,1,0:T(8,128)}, u32[]{:S(2)}) copy-start(f32[1,1,1024,512]{3,2,1,0:T(8,128)} %param.8) | copy-start | bytes 6291460
  22.2 0.8 copy-start.8
  23.0 18.0 %all-to-all-start = ((bf16[4,128,1024]{2,1,0:T(8,128)(2,1)}), bf16[4,128,1024]{2,1,0:T(8,128)(2,1)S(1)}, u32[]{:S(2)}, u32[]{:S(2)}) async-start(bf16[4,128,1024]{2,1,0:T(8,128)(2,1)} %bitcast.128), calls=%async_computation | async-start | bytes 2097152 | tf_op jit(solution)/shard_map/all_to_all | solution.py:72
  40.9 2.1 copy-start.7
  43.0 2.7 %copy-start.4 = (bf16[512,512]{1,0:T(8,128)(2,1)}, bf16[512,512]{1,0:T(8,128)(2,1)S(1)}, u32[]{:S(2)}) copy-start(bf16[512,512]{1,0:T(8,128)(2,1)S(1)} %fusion.17) | copy-start | bytes 1572868
  61.6 18.0 %copy-start.12 = (bf16[2,256,512]{2,1,0:T(8,128)(2,1)S(1)}, bf16[2,256,512]{2,1,0:T(8,128)(2,1)}, u32[]{:S(2)}) copy-start(bf16[2,256,512]{2,1,0:T(8,128)(2,1)} %param.7) | copy-start | bytes 1572868
  66.1 62.6 %collective-permute-start = (bf16[1024,512]{1,0:T(8,128)(2,1)}, bf16[1024,512]{1,0:T(8,128)(2,1)}, u32[]{:S(2)}, u32[]{:S(2)}) collective-permute-start(bf16[1024,512]{1,0:T(8,128)(2,1)} %get-tuple-element.9), channel_id=1, source_target_pairs={{63,0},{0,1},{1,2},{2,3},{3,4},{4,5},{5,6},{6,7},{7,8},{8,9},{9,10... | collective-permute-start | bytes 3145736 | tf_op jit(solution)/shard_map/ppermute | solution.py:15
  67.1 61.6 %collective-permute-start.1 = (bf16[1024,512]{1,0:T(8,128)(2,1)}, bf16[1024,512]{1,0:T(8,128)(2,1)}, u32[]{:S(2)}, u32[]{:S(2)}) collective-permute-start(bf16[1024,512]{1,0:T(8,128)(2,1)} %get-tuple-element.9), channel_id=1, source_target_pairs={{1,0},{2,1},{3,2},{4,3},{5,4},{6,5},{7,6},{8,7},{9,8},{10,9},{11,1... | collective-permute-start | bytes 3145736 | tf_op jit(solution)/shard_map/ppermute | solution.py:15
  74.8 53.8 %collective-permute-start.2 = (bf16[1024,512]{1,0:T(8,128)(2,1)}, bf16[1024,512]{1,0:T(8,128)(2,1)}, u32[]{:S(2)}, u32[]{:S(2)}) collective-permute-start(bf16[1024,512]{1,0:T(8,128)(2,1)} %get-tuple-element.9), channel_id=1, source_target_pairs={{62,0},{63,1},{0,2},{1,3},{2,4},{3,5},{4,6},{5,7},{6,8},{7,9},{8,1... | collective-permute-start | bytes 3145736 | tf_op jit(solution)/shard_map/ppermute | solution.py:15
  74.8 59.8 %collective-permute-start.3 = (bf16[1024,512]{1,0:T(8,128)(2,1)}, bf16[1024,512]{1,0:T(8,128)(2,1)}, u32[]{:S(2)}, u32[]{:S(2)}) collective-permute-start(bf16[1024,512]{1,0:T(8,128)(2,1)} %get-tuple-element.9), channel_id=1, source_target_pairs={{2,0},{3,1},{4,2},{5,3},{6,4},{7,5},{8,6},{9,7},{10,8},{11,9},{12,... | collective-permute-start | bytes 3145736 | tf_op jit(solution)/shard_map/ppermute | solution.py:15
  80.8 37.1 %all-to-all-start.3 = ((bf16[4,128,512]{2,1,0:T(8,128)(2,1)}), bf16[4,128,512]{2,1,0:T(8,128)(2,1)S(1)}, u32[]{:S(2)}, u32[]{:S(2)}) async-start(bf16[4,128,512]{2,1,0:T(8,128)(2,1)} %bitcast.25), calls=%async_computation.3 | async-start | bytes 1048576 | tf_op jit(solution)/shard_map/all_to_all | solution.py:75
  117.9 0.8 copy-start.9
  118.7 18.9 %all-to-all-start.2 = ((bf16[4,128,1024]{2,1,0:T(8,128)(2,1)}), bf16[4,128,1024]{2,1,0:T(8,128)(2,1)S(1)}, u32[]{:S(2)}, u32[]{:S(2)}) async-start(bf16[4,128,1024]{2,1,0:T(8,128)(2,1)} %bitcast.127), calls=%async_computation.2 | async-start | bytes 2097152 | tf_op jit(solution)/shard_map/all_to_all | solution.py:72
  125.7 8.9 %copy-start.2 = (f32[1024,512]{1,0:T(8,128)S(1)}, f32[1024,512]{1,0:T(8,128)}, u32[]{:S(2)}) copy-start(f32[1024,512]{1,0:T(8,128)} %get-tuple-element.10) | copy-start | bytes 6291460
  137.6 28.2 %all-to-all-start.4 = ((bf16[4,128,1024]{2,1,0:T(8,128)(2,1)}), bf16[4,128,1024]{2,1,0:T(8,128)(2,1)}, u32[]{:S(2)}, u32[]{:S(2)}) async-start(bf16[4,128,1024]{2,1,0:T(8,128)(2,1)} %bitcast.125), calls=%async_computation.4 | async-start | bytes 2097152 | tf_op jit(solution)/shard_map/all_to_all | solution.py:99
  143.6 2.1 copy-start.1
  145.7 2.7 %copy-start.5 = (bf16[512,512]{1,0:T(8,128)(2,1)}, bf16[512,512]{1,0:T(8,128)(2,1)S(1)}, u32[]{:S(2)}) copy-start(bf16[512,512]{1,0:T(8,128)(2,1)S(1)} %fusion.16) | copy-start | bytes 1572868
  156.6 1.0 copy-start.13
  162.5 1.6 copy-start.10
  162.5 1.5 copy-start.6
  165.7 40.9 %all-to-all-start.5 = ((bf16[4,128,1024]{2,1,0:T(8,128)(2,1)}), bf16[4,128,1024]{2,1,0:T(8,128)(2,1)S(1)}, u32[]{:S(2)}, u32[]{:S(2)}) async-start(bf16[4,128,1024]{2,1,0:T(8,128)(2,1)} %bitcast.32), calls=%async_computation.5 | async-start | bytes 2097152 | tf_op jit(solution)/shard_map/all_to_all | solution.py:99
  174.2 64.3 %collective-permute-start.4 = (bf16[1024,512]{1,0:T(8,128)(2,1)}, bf16[1024,512]{1,0:T(8,128)(2,1)}, u32[]{:S(2)}, u32[]{:S(2)}) collective-permute-start(bf16[1024,512]{1,0:T(8,128)(2,1)} %get-tuple-element.13), channel_id=1, source_target_pairs={{63,0},{0,1},{1,2},{2,3},{3,4},{4,5},{5,6},{6,7},{7,8},{8,9},{9,10... | collective-permute-start | bytes 3145736 | tf_op jit(solution)/shard_map/ppermute | solution.py:15
  193.2 45.5 %collective-permute-start.5 = (bf16[1024,512]{1,0:T(8,128)(2,1)}, bf16[1024,512]{1,0:T(8,128)(2,1)}, u32[]{:S(2)}, u32[]{:S(2)}) collective-permute-start(bf16[1024,512]{1,0:T(8,128)(2,1)} %get-tuple-element.13), channel_id=1, source_target_pairs={{1,0},{2,1},{3,2},{4,3},{5,4},{6,5},{7,6},{8,7},{9,8},{10,9},{11,1... | collective-permute-start | bytes 3145736 | tf_op jit(solution)/shard_map/ppermute | solution.py:15
  193.3 45.5 %collective-permute-start.6 = (bf16[1024,512]{1,0:T(8,128)(2,1)}, bf16[1024,512]{1,0:T(8,128)(2,1)}, u32[]{:S(2)}, u32[]{:S(2)}) collective-permute-start(bf16[1024,512]{1,0:T(8,128)(2,1)} %get-tuple-element.13), channel_id=1, source_target_pairs={{62,0},{63,1},{0,2},{1,3},{2,4},{3,5},{4,6},{5,7},{6,8},{7,9},{8,1... | collective-permute-start | bytes 3145736 | tf_op jit(solution)/shard_map/ppermute | solution.py:15
  194.4 54.4 %collective-permute-start.7 = (bf16[1024,512]{1,0:T(8,128)(2,1)}, bf16[1024,512]{1,0:T(8,128)(2,1)}, u32[]{:S(2)}, u32[]{:S(2)}) collective-permute-start(bf16[1024,512]{1,0:T(8,128)(2,1)} %get-tuple-element.13), channel_id=1, source_target_pairs={{2,0},{3,1},{4,2},{5,3},{6,4},{7,5},{8,6},{9,7},{10,8},{11,9},{12,... | collective-permute-start | bytes 3145736 | tf_op jit(solution)/shard_map/ppermute | solution.py:15
  206.6 42.3 %copy-start.3 = (f32[1024,512]{1,0:T(8,128)S(1)}, f32[1024,512]{1,0:T(8,128)}, u32[]{:S(2)}) copy-start(f32[1024,512]{1,0:T(8,128)} %get-tuple-element.14) | copy-start | bytes 6291460
where the time goes:
time: 257 us; the launch traced here: 253 us
  waiting for transfers between devices  93 us (36%)
  starting transfers between devices  74 us (29%)
  matrix products  62.7 us (24%)
  other arithmetic  17.2 us (7%)
  local copies, waits for them, and re-layouts  3.98 us (2%)
    ppermute x8, waiting for transfers between devices, shifted(): return lax.ppermute(block, axis, route)  45.5 us
    ppermute x8, starting transfers between devices, shifted(): return lax.ppermute(block, axis, route)  43.4 us
    all_to_all x2, waiting for transfers between devices, on_device(): lax.all_to_all(sent_grads[round_index], 'expert', split_axis=0, concat_ax...  36.1 us
    dot_general x6, matrix products, orthogonalize(): jnp.dot(orthog, polynom, preferred_element_type=jnp.float32)  24 us
    dot_general x6, matrix products, orthogonalize(): lax.dot_general(orthog, orthog, (((0,), (0,)), ((), ())), preferred_eleme...  14.4 us
    all_to_all x2, starting transfers between devices, on_device(): lax.all_to_all(sent_grads[round_index], 'expert', split_axis=0, concat_ax...  11.8 us
    all_to_all x2, waiting for transfers between devices, on_device(): lax.all_to_all(sent_rows[round_index], 'expert', split_axis=0, concat_axi...  11.4 us
    all_to_all x2, starting transfers between devices, on_device(): lax.all_to_all(backward, 'expert', split_axis=0, concat_axis=0, tiled=True)  9.54 us
  transfers between devices with their start and end apart: 14, of which 7 were waited for; matrix products, arithmetic and copies ran while one was open for 18% of the time, Pallas kernels for 0%

commit v1 on v0

--- a/solution.py
+++ b/solution.py
@@ -9,16 +9,14 @@
 NS_STEPS = 3
 
 
-def shifted(block, axis, distance):
-    devices = range(lax.axis_size(axis))
-    route = [((i - distance) % len(devices), i) for i in devices]
-    return lax.ppermute(block, axis, route)
-
-
 def dispatch_table(route, experts_all, capacity):
+    rows = route.shape[0]
     labels = jnp.arange(experts_all, dtype=jnp.int32)
-    onehot = (route[:, None] == labels[None, :]).astype(jnp.int32)
-    slot_rank = jnp.sum(onehot * (jnp.cumsum(onehot, axis=0) - 1), axis=1)
+    onehot = (route[:, None] == labels[None, :])
+    places = jnp.arange(rows, dtype=jnp.int32)
+    earlier = (places[:, None] > places[None, :]).astype(jnp.bfloat16)
+    ranks = jnp.dot(earlier, onehot.astype(jnp.bfloat16), preferred_element_type=jnp.float32)
+    slot_rank = jnp.sum(jnp.where(onehot, ranks, 0.0), axis=1).astype(jnp.int32)
     target = route * capacity + slot_rank
     slot_ids = jnp.arange(experts_all * capacity, dtype=jnp.int32)
     return (slot_ids[:, None] == target[None, :]).astype(jnp.bfloat16)
@@ -40,6 +38,17 @@
     return orthog
 
 
+def neighbour_sum(shared):
+    nodes = lax.axis_size("node")
+    below = lax.ppermute(shared, "node", [((i - 2) % nodes, i) for i in range(nodes)])
+    above = lax.ppermute(shared, "node", [((i + 2) % nodes, i) for i in range(nodes)])
+    even = lax.axis_index("node") % 2 == 0
+    beside = jnp.where(even, above, below)
+    pair = (shared.astype(jnp.float32) + beside.astype(jnp.float32)).astype(jnp.bfloat16)
+    across = lax.ppermute(pair, "node", [(i ^ 1, i) for i in range(nodes)])
+    return below.astype(jnp.float32) + above.astype(jnp.float32) + across.astype(jnp.float32)
+
+
 def on_device(tokens, routing, out_grad, weights, momentum):
     row_count = tokens.shape[1]
     model_width = tokens.shape[2]
@@ -51,33 +60,18 @@
     weight = weights[0, 0]
     moment = momentum[0, 0]
     tables = []
-    sent_rows = []
-    sent_grads = []
+    received = []
     for round_index in range(ROUNDS):
         dispatch = dispatch_table(routing[round_index], experts_all, capacity)
         tables.append(dispatch)
-        sent_rows.append(
-            jnp.dot(dispatch, tokens[round_index], preferred_element_type=jnp.float32)
-            .astype(jnp.bfloat16)
-            .reshape(experts_all, capacity, model_width)
-        )
-        sent_grads.append(
-            jnp.dot(dispatch, out_grad[round_index], preferred_element_type=jnp.float32)
-            .astype(jnp.bfloat16)
-            .reshape(experts_all, capacity, hidden_width)
-        )
+        rows = jnp.concatenate([tokens[round_index], out_grad[round_index]], axis=1)
+        sent = jnp.dot(dispatch, rows, preferred_element_type=jnp.float32)
+        sent = sent.astype(jnp.bfloat16).reshape(experts_all, capacity, -1)
+        received.append(lax.all_to_all(sent, "expert", split_axis=0, concat_axis=0, tiled=True))
     in_grads = []
     for round_index in range(ROUNDS):
-        got_rows, got_grads = (
-            lax.all_to_all(
-                sent_rows[round_index], "expert", split_axis=0, concat_axis=0, tiled=True
-            ),
-            lax.all_to_all(
-                sent_grads[round_index], "expert", split_axis=0, concat_axis=0, tiled=True
-            ),
-        )
-        got_rows = got_rows.reshape(-1, model_width)
-        got_grads = got_grads.reshape(-1, hidden_width)
+        got = received[round_index].reshape(-1, model_width + hidden_width)
+        got_rows, got_grads = got[:, :model_width], got[:, model_width:]
         shaped = weight.astype(jnp.bfloat16)
         preact = jnp.dot(got_rows, shaped, preferred_element_type=jnp.float32) * factor
         slopes = (got_grads.astype(jnp.float32) * 2.0 * jnp.maximum(preact, 0.0)).astype(
@@ -110,14 +104,7 @@
         moment = 0.9 * moment + grad_w
         orthog = orthogonalize(moment)
         stepped = weight - step_size * orthog.astype(jnp.float32)
-        shared = stepped.astype(jnp.bfloat16)
-        near_left = shifted(shared, "node", 1)
-        near_right = shifted(shared, "node", -1)
-        far_left = shifted(shared, "node", 2)
-        far_right = shifted(shared, "node", -2)
-        neighbours = near_left.astype(jnp.float32) + near_right.astype(jnp.float32)
-        neighbours = neighbours + far_left.astype(jnp.float32) + far_right.astype(jnp.float32)
-        weight = 0.4 * stepped + 0.15 * neighbours
+        weight = 0.4 * stepped + 0.15 * neighbour_sum(stepped.astype(jnp.bfloat16))
     return (weight[None, None], moment[None, None], jnp.stack(in_grads))
 
 

time: 257 us -> 229 us (0.89); the launches traced: 253 us -> 228 us
  starting transfers between devices: 74 us -> 32.1 us
  blocking collectives: 0 us -> 24.9 us
  waiting for transfers between devices: 93 us -> 88.4 us
  other arithmetic: 17.2 us -> 12.8 us
  local copies, waits for them, and re-layouts: 3.98 us -> 6.71 us
    all_to_all x4 -> x1, waiting for transfers between devices: 47.5 us -> 13.6 us  [on_device(): lax.all_to_all(sent, 'expert', split_axis=0, concat_axis=0, tiled=True)]
    ppermute x8 -> x6, starting transfers between devices: 43.4 us -> 13.9 us  [the longest x2 11.2 us: neighbour_sum(): lax.ppermute(shared, 'node', [((i + 2) % nodes, i) for i in range(nodes)])]
    all_to_all x0 -> x1, blocking collectives: none -> 24.9 us  [on_device(): lax.all_to_all(sent, 'expert', split_axis=0, concat_axis=0, tiled=True)]
    all_to_all x2, waiting for transfers between devices: 0.01 us -> 19 us  [on_device(): lax.all_to_all(backward, 'expert', split_axis=0, concat_axis=0, tiled=True)]
    all_to_all x4 -> x1, starting transfers between devices: 21 us -> 6.22 us  [on_device(): lax.all_to_all(sent, 'expert', split_axis=0, concat_axis=0, tiled=True)]
    ppermute x8 -> x6, waiting for transfers between devices: 45.5 us -> 55.8 us  [the longest x2 33.3 us: neighbour_sum(): across = lax.ppermute(pair, 'node', [(i ^ 1, i) for i in range(nodes)])]
    convert_element_type x2 -> x4, other arithmetic: 0.01 us -> 4.43 us  [the longest x2 4.42 us: neighbour_sum(): (shared.astype(jnp.float32) + beside.astype(jnp.float32)).astype(jnp.bflo...]
    dot_general x4, matrix products: 7.06 us -> 2.7 us  [the longest x2 2.31 us: on_device(): sent = jnp.dot(dispatch, rows, preferred_element_type=jnp.float32)]
  transfers between devices with their start and end apart: 14 -> 9, of which waited for: 7 -> 6; matrix products, arithmetic and copies ran while one was open for 18% -> 9% of each run, Pallas kernels for 0% -> 0%
where the time goes in v1:
time: 229 us; the launch traced here: 228 us
  waiting for transfers between devices  88.4 us (39%)
  matrix products  61 us (27%)
  starting transfers between devices  32.1 us (14%)
  blocking collectives  24.9 us (11%)
  other arithmetic  12.8 us (6%)
  local copies, waits for them, and re-layouts  6.71 us (3%)
    ppermute x2, waiting for transfers between devices, neighbour_sum(): across = lax.ppermute(pair, 'node', [(i ^ 1, i) for i in range(nodes)])  33.3 us
    all_to_all x1, blocking collectives, on_device(): lax.all_to_all(sent, 'expert', split_axis=0, concat_axis=0, tiled=True)  24.9 us
    dot_general x6, matrix products, orthogonalize(): jnp.dot(orthog, polynom, preferred_element_type=jnp.float32)  23.4 us
    ppermute x2, waiting for transfers between devices, neighbour_sum(): lax.ppermute(shared, 'node', [((i - 2) % nodes, i) for i in range(nodes)])  22.5 us
    all_to_all x2, waiting for transfers between devices, on_device(): lax.all_to_all(backward, 'expert', split_axis=0, concat_axis=0, tiled=True)  19 us
    dot_general x6, matrix products, orthogonalize(): lax.dot_general(orthog, orthog, (((0,), (0,)), ((), ())), preferred_eleme...  14.6 us
    all_to_all x1, waiting for transfers between devices, on_device(): lax.all_to_all(sent, 'expert', split_axis=0, concat_axis=0, tiled=True)  13.6 us
    all_to_all x2, starting transfers between devices, on_device(): lax.all_to_all(backward, 'expert', split_axis=0, concat_axis=0, tiled=True)  12 us
  transfers between devices with their start and end apart: 9, of which 6 were waited for; matrix products, arithmetic and copies ran while one was open for 9% of the time, Pallas kernels for 0%

profile of v1, /device:TPU:1, one launch (start us, length us, event | category | flops | bytes accessed | tf_op | source)
XLA Modules:
  0.0 228.1 jit_solution(11971693842118387684)
XLA Ops:
  0.6 0.0 copy-start.12
  0.6 0.0 copy-start.11
  0.7 0.8 fusion.80
  1.5 0.2 fusion.21
  1.7 0.2 fusion.20
  1.9 2.1 slice_bitcast_fusion
  4.0 0.0 copy-done.11
  4.0 0.0 copy-done.12
  4.0 0.6 convolution_convert_fusion.1
  4.6 0.0 copy-start
  4.6 24.9 %all_to_all.20 = bf16[4,128,1536]{2,1,0:T(8,128)(2,1)S(1)} all-to-all(bf16[4,128,1536]{2,1,0:T(8,128)(2,1)S(1)} %bitcast.84), channel_id=1, replica_groups=mesh['expert'=4,'node'=64] {'expert'}, dimensions={0} | all-to-all | bytes 3145728 | tf_op jit(solution)/shard_map/all_to_all | solution.py:70
  29.5 0.0 copy-done
  29.5 0.8 fusion.17
  30.3 0.8 copy-done.13
  31.1 2.7 %multiply_reduce_fusion.1 = (f32[]{:T(128)}, f32[1024,512]{1,0:T(8,128)}) fusion(bf16[512,512]{1,0:T(8,128)(2,1)S(1)} %fusion.17, bf16[512,1536]{1,0:T(8,128)(2,1)S(1)} %bitcast.88, f32[1,1,1024,512]{3,2,1,0:T(8,128)S(1)} %copy-done.13), kind=kOutput, calls=%fused_computation.22 | convolution fusion | flops 539492352 | bytes 5767172 | tf_op jit(solution)/shard_map/dot_general | solution.py:88
  33.8 0.0 copy-done.9
  34.5 3.8 %convolution_convert_fusion.9 = bf16[512,512]{1,0:T(8,128)(2,1)} fusion(f32[1024,512]{1,0:T(8,128)} %get-tuple-element.12, f32[]{:T(128)S(6)} %add.87), kind=kOutput, calls=%fused_computation.56 | convolution fusion | flops 538181632 | bytes 2621444 | tf_op jit(solution)/shard_map/dot_general | solution.py:29
  38.2 3.8 %add_convert_fusion.7 = bf16[1024,512]{1,0:T(8,128)(2,1)S(1)} fusion(bf16[512,512]{1,0:T(8,128)(2,1)} %convolution_convert_fusion.9, f32[1024,512]{1,0:T(8,128)} %get-tuple-element.12, f32[]{:T(128)S(6)} %add.87), kind=kOutput, calls=%fused_computation.20 | convolution fusion | flops 810811392 | bytes 3670020 | tf_op jit(solution)/shard_map/dot_general | solution.py:36
  42.0 0.0 copy-start.15
  42.0 1.0 copy-done.15
  43.0 1.5 convolution_convert_fusion.8
  44.5 3.2 %add_convert_fusion.6 = bf16[1024,512]{1,0:T(8,128)(2,1)S(1)} fusion(bf16[1024,512]{1,0:T(8,128)(2,1)} %copy-done.15, bf16[512,512]{1,0:T(8,128)(2,1)} %convolution_convert_fusion.8), kind=kOutput, calls=%fused_computation.19 | convolution fusion | flops 808714240 | bytes 2621440 | tf_op jit(solution)/shard_map/dot_general | solution.py:36
  47.8 0.0 copy-start.8
  47.8 1.0 copy-done.8
  48.7 1.5 convolution_convert_fusion.7
  50.3 4.7 %fusion.81 = (bf16[1024,512]{1,0:T(8,128)(2,1)S(1)}, f32[1024,512]{1,0:T(8,128)}) fusion(bf16[1024,512]{1,0:T(8,128)(2,1)} %copy-done.8, bf16[512,512]{1,0:T(8,128)(2,1)} %convolution_convert_fusion.7, f32[1,1,1024,512]{3,2,1,0:T(8,128)S(1)} %copy-done), kind=kOutput, calls=%fused_computation.132 | convolution fusion | flops 810811392 | bytes 6815744 | tf_op jit(solution)/shard_map/dot_general | solution.py:36
  55.0 0.0 collective-permute-start
  55.0 6.4 %collective-permute-start.1 = (bf16[1024,512]{1,0:T(8,128)(2,1)S(1)}, bf16[1024,512]{1,0:T(8,128)(2,1)S(1)}, u32[]{:S(2)}, u32[]{:S(2)}) collective-permute-start(bf16[1024,512]{1,0:T(8,128)(2,1)S(1)} %get-tuple-element.13), channel_id=1, source_target_pairs={{2,0},{3,1},{4,2},{5,3},{6,4},{7,5},{8,6},{9,7},{10,8},{11,9},{12,... | collective-permute-start | bytes 3145736 | tf_op jit(solution)/shard_map/ppermute | solution.py:44
  61.4 22.5 %collective-permute-done = bf16[1024,512]{1,0:T(8,128)(2,1)S(1)} collective-permute-done((bf16[1024,512]{1,0:T(8,128)(2,1)S(1)}, bf16[1024,512]{1,0:T(8,128)(2,1)S(1)}, u32[]{:S(2)}, u32[]{:S(2)}) %collective-permute-start) | collective-permute-done | bytes 1048608 | tf_op jit(solution)/shard_map/ppermute | solution.py:43
  83.8 0.0 collective-permute-done.1
  83.8 1.4 add_convert_fusion.4
  85.3 2.6 %collective-permute-start.2 = (bf16[1024,512]{1,0:T(8,128)(2,1)}, bf16[1024,512]{1,0:T(8,128)(2,1)S(1)}, u32[]{:S(2)}, u32[]{:S(2)}) collective-permute-start(bf16[1024,512]{1,0:T(8,128)(2,1)} %add_convert_fusion.4), channel_id=1, source_target_pairs={{1,0},{0,1},{3,2},{2,3},{5,4},{4,5},{7,6},{6,7},{9,8},{8,9},{11,10... | collective-permute-start | bytes 3145736 | tf_op jit(solution)/shard_map/ppermute | solution.py:48
  87.9 1.7 convolution_convert_fusion
  89.6 6.2 %all-to-all-start.1 = ((bf16[4,128,1536]{2,1,0:T(8,128)(2,1)}), bf16[4,128,1536]{2,1,0:T(8,128)(2,1)}, u32[]{:S(2)}, u32[]{:S(2)}) async-start(bf16[4,128,1536]{2,1,0:T(8,128)(2,1)} %bitcast.14), calls=%async_computation.1 | async-start | bytes 3145728 | tf_op jit(solution)/shard_map/all_to_all | solution.py:70
  95.8 14.1 %collective-permute-done.2 = bf16[1024,512]{1,0:T(8,128)(2,1)S(1)} collective-permute-done((bf16[1024,512]{1,0:T(8,128)(2,1)}, bf16[1024,512]{1,0:T(8,128)(2,1)S(1)}, u32[]{:S(2)}, u32[]{:S(2)}) %collective-permute-start.2) | collective-permute-done | bytes 1048608 | tf_op jit(solution)/shard_map/ppermute | solution.py:48
  110.0 1.0 copy-done.7
  111.0 2.8 %multiply_add_fusion.1 = f32[1024,512]{1,0:T(8,128)S(1)} fusion(bf16[1024,512]{1,0:T(8,128)(2,1)} %copy-done.7, bf16[1024,512]{1,0:T(8,128)(2,1)} %copy-done.2, bf16[1024,512]{1,0:T(8,128)(2,1)S(1)} %collective-permute-done, f32[1024,512]{1,0:T(8,128)} %get-tuple-element.14), kind=kLoop, calls=%fused_computation.16 | loop fusion | flops 4194304 | bytes 7340032 | tf_op jit(solution)/shard_map/add | solution.py:107
  113.8 13.6 %all-to-all-done.1 = bf16[4,128,1536]{2,1,0:T(8,128)(2,1)} async-done(((bf16[4,128,1536]{2,1,0:T(8,128)(2,1)}), bf16[4,128,1536]{2,1,0:T(8,128)(2,1)}, u32[]{:S(2)}, u32[]{:S(2)}) %all-to-all-start.1) | async-done | bytes 1572896 | tf_op jit(solution)/shard_map/all_to_all | solution.py:70
  127.4 2.2 fusion.16
  129.7 4.1 %multiply_reduce_fusion = (f32[]{:T(128)}, f32[1024,512]{1,0:T(8,128)}) fusion(bf16[512,512]{1,0:T(8,128)(2,1)S(1)} %fusion.16, bf16[512,1536]{1,0:T(8,128)(2,1)} %bitcast.15, f32[1024,512]{1,0:T(8,128)S(1)} %copy-done.14), kind=kOutput, calls=%fused_computation.14 | convolution fusion | flops 539492352 | bytes 5767172 | tf_op jit(solution)/shard_map/dot_general | solution.py:88
  134.5 3.8 %convolution_convert_fusion.6 = bf16[512,512]{1,0:T(8,128)(2,1)} fusion(f32[1024,512]{1,0:T(8,128)} %get-tuple-element.16, f32[]{:T(128)S(6)} %add.101), kind=kOutput, calls=%fused_computation.53 | convolution fusion | flops 538181632 | bytes 2621444 | tf_op jit(solution)/shard_map/dot_general | solution.py:29
  138.3 3.8 %add_convert_fusion.3 = bf16[1024,512]{1,0:T(8,128)(2,1)S(1)} fusion(bf16[512,512]{1,0:T(8,128)(2,1)} %convolution_convert_fusion.6, f32[1024,512]{1,0:T(8,128)} %get-tuple-element.16, f32[]{:T(128)S(6)} %add.101), kind=kOutput, calls=%fused_computation.12 | convolution fusion | flops 810811392 | bytes 3670020 | tf_op jit(solution)/shard_map/dot_general | solution.py:36
  142.1 1.5 convolution_convert_fusion.5
  143.7 3.4 %add_convert_fusion.2 = bf16[1024,512]{1,0:T(8,128)(2,1)} fusion(bf16[1024,512]{1,0:T(8,128)(2,1)S(1)} %add_convert_fusion.3, bf16[512,512]{1,0:T(8,128)(2,1)} %convolution_convert_fusion.5), kind=kOutput, calls=%fused_computation.11 | convolution fusion | flops 808714240 | bytes 2621440 | tf_op jit(solution)/shard_map/dot_general | solution.py:36
  147.1 2.4 %convolution_convert_fusion.4 = bf16[512,512]{1,0:T(8,128)(2,1)S(1)} fusion(bf16[1024,512]{1,0:T(8,128)(2,1)} %add_convert_fusion.2), kind=kOutput, calls=%fused_computation.51 | convolution fusion | flops 537133056 | bytes 1572864 | tf_op jit(solution)/shard_map/dot_general | solution.py:29
  149.5 4.5 %fusion.82 = (bf16[1024,512]{1,0:T(8,128)(2,1)}, f32[1024,512]{1,0:T(8,128)}) fusion(f32[1024,512]{1,0:T(8,128)S(1)} %multiply_add_fusion.1, bf16[1024,512]{1,0:T(8,128)(2,1)} %add_convert_fusion.2, bf16[512,512]{1,0:T(8,128)(2,1)S(1)} %convolution_convert_fusion.4), kind=kOutput, calls=%fused_computation.133 | convolution fusion | flops 810811392 | bytes 6815744 | tf_op jit(solution)/shard_map/dot_general | solution.py:36
  154.0 0.0 collective-permute-start.3
  154.0 4.8 %collective-permute-start.4 = (bf16[1024,512]{1,0:T(8,128)(2,1)}, bf16[1024,512]{1,0:T(8,128)(2,1)}, u32[]{:S(2)}, u32[]{:S(2)}) collective-permute-start(bf16[1024,512]{1,0:T(8,128)(2,1)} %get-tuple-element.17), channel_id=1, source_target_pairs={{2,0},{3,1},{4,2},{5,3},{6,4},{7,5},{8,6},{9,7},{10,8},{11,9},{12,... | collective-permute-start | bytes 3145736 | tf_op jit(solution)/shard_map/ppermute | solution.py:44
  158.8 3.5 %multiply_convert_fusion.1 = bf16[512,1024]{1,0:T(8,128)(2,1)} fusion(bf16[512,512]{1,0:T(8,128)(2,1)} %copy-done.9, f32[1,1,1024,512]{3,2,1,0:T(8,128)} %param.8), kind=kOutput, calls=%fused_computation.6 | convolution fusion | flops 537919488 | bytes 3670016 | tf_op jit(solution)/shard_map/dot_general | solution.py:81
  162.3 6.9 %all-to-all-start.2 = ((bf16[4,128,1024]{2,1,0:T(8,128)(2,1)}), bf16[4,128,1024]{2,1,0:T(8,128)(2,1)}, u32[]{:S(2)}, u32[]{:S(2)}) async-start(bf16[4,128,1024]{2,1,0:T(8,128)(2,1)} %bitcast.86), calls=%async_computation.2 | async-start | bytes 2097152 | tf_op jit(solution)/shard_map/all_to_all | solution.py:93
  169.1 2.8 %multiply_convert_fusion = bf16[512,1024]{1,0:T(8,128)(2,1)} fusion(bf16[512,512]{1,0:T(8,128)(2,1)} %copy-done.10, f32[1024,512]{1,0:T(8,128)S(1)} %multiply_add_fusion.1), kind=kOutput, calls=%fused_computation.5 | convolution fusion | flops 538443776 | bytes 3670016 | tf_op jit(solution)/shard_map/dot_general | solution.py:81
  171.9 10.9 %all-to-all-done.2 = bf16[4,128,1024]{2,1,0:T(8,128)(2,1)} async-done(((bf16[4,128,1024]{2,1,0:T(8,128)(2,1)}), bf16[4,128,1024]{2,1,0:T(8,128)(2,1)}, u32[]{:S(2)}, u32[]{:S(2)}) %all-to-all-start.2) | async-done | bytes 1048608 | tf_op jit(solution)/shard_map/all_to_all | solution.py:93
  182.8 5.1 %all-to-all-start.3 = ((bf16[4,128,1024]{2,1,0:T(8,128)(2,1)}), bf16[4,128,1024]{2,1,0:T(8,128)(2,1)}, u32[]{:S(2)}, u32[]{:S(2)}) async-start(bf16[4,128,1024]{2,1,0:T(8,128)(2,1)} %bitcast.85), calls=%async_computation.3 | async-start | bytes 2097152 | tf_op jit(solution)/shard_map/all_to_all | solution.py:93
  187.9 0.0 collective-permute-done.3
  187.9 0.0 collective-permute-done.4
  188.0 3.0 %add_convert_fusion = bf16[1024,512]{1,0:T(8,128)(2,1)} fusion(bf16[1024,512]{1,0:T(8,128)(2,1)S(1)} %copy-done.5, bf16[1024,512]{1,0:T(8,128)(2,1)} %collective-permute-done.4, bf16[1024,512]{1,0:T(8,128)(2,1)S(1)} %collective-permute-done.3, pred[]{:T(512)S(6)} %eq.75), kind=kLoop, calls=%fused_computation.8 | loop fusion | flops 2621440 | bytes 4194305 | tf_op jit(solution)/shard_map/convert_element_type | solution.py:47
  191.0 0.0 copy-done.3
  191.0 0.1 collective-permute-start.5
  191.0 2.5 %fusion.18 = bf16[1,256,1024]{2,1,0:T(8,128)(2,1)} fusion(bf16[512,1024]{1,0:T(8,128)(2,1)} %bitcast.19, s32[256]{0:T(256)S(1)} %bitcast.92), kind=kOutput, calls=%fused_computation.57 | convolution fusion | flops 268828672 | bytes 1573888 | tf_op jit(solution)/shard_map/dot_general | solution.py:97
  193.6 8.1 %all-to-all-done.3 = bf16[4,128,1024]{2,1,0:T(8,128)(2,1)} async-done(((bf16[4,128,1024]{2,1,0:T(8,128)(2,1)}), bf16[4,128,1024]{2,1,0:T(8,128)(2,1)}, u32[]{:S(2)}, u32[]{:S(2)}) %all-to-all-start.3) | async-done | bytes 1048608 | tf_op jit(solution)/shard_map/all_to_all | solution.py:93
  201.6 1.7 fusion.19
  203.4 2.1 pad_maximum_fusion
  205.5 19.2 %collective-permute-done.5 = bf16[1024,512]{1,0:T(8,128)(2,1)} collective-permute-done((bf16[1024,512]{1,0:T(8,128)(2,1)}, bf16[1024,512]{1,0:T(8,128)(2,1)}, u32[]{:S(2)}, u32[]{:S(2)}) %collective-permute-start.5) | collective-permute-done | bytes 1048608 | tf_op jit(solution)/shard_map/ppermute | solution.py:48
  224.6 3.5 %add_bitcast_fusion = f32[1,1,1024,512]{3,2,1,0:T(8,128)} fusion(bf16[1024,512]{1,0:T(8,128)(2,1)} %collective-permute-done.5, bf16[1024,512]{1,0:T(8,128)(2,1)} %collective-permute-done.4, bf16[1024,512]{1,0:T(8,128)(2,1)S(1)} %copy-done.4, f32[1024,512]{1,0:T(8,128)S(1)} %copy-done.1), kind=kLoop, calls=%fused_computation.7 | loop fusion | flops 4194304 | bytes 7340032 | tf_op jit(solution)/shard_map/broadcast_in_dim | solution.py:108
  (22 shorter events, 0.1 us)
Async XLA Ops:
  0.6 3.4 %copy-start.12 = (s32[2,256]{1,0:T(2,128)S(1)}, s32[2,256]{1,0:T(2,128)}, u32[]{:S(2)}) copy-start(s32[2,256]{1,0:T(2,128)} %param.6) | copy-start | bytes 6148
  0.6 3.3 %copy-start.11 = (bf16[2,256,512]{2,1,0:T(8,128)(2,1)S(1)}, bf16[2,256,512]{2,1,0:T(8,128)(2,1)}, u32[]{:S(2)}) copy-start(bf16[2,256,512]{2,1,0:T(8,128)(2,1)} %param.7) | copy-start | bytes 1572868
  4.6 24.9 %copy-start = (f32[1,1,1024,512]{3,2,1,0:T(8,128)S(1)}, f32[1,1,1024,512]{3,2,1,0:T(8,128)}, u32[]{:S(2)}) copy-start(f32[1,1,1024,512]{3,2,1,0:T(8,128)} %param.8) | copy-start | bytes 6291460
  29.5 1.6 copy-start.13
  31.1 2.7 %copy-start.9 = (bf16[512,512]{1,0:T(8,128)(2,1)}, bf16[512,512]{1,0:T(8,128)(2,1)S(1)}, u32[]{:S(2)}) copy-start(bf16[512,512]{1,0:T(8,128)(2,1)S(1)} %fusion.17) | copy-start | bytes 1572868
  42.0 1.0 copy-start.15
  47.8 1.0 copy-start.8
  55.0 28.9 %collective-permute-start = (bf16[1024,512]{1,0:T(8,128)(2,1)S(1)}, bf16[1024,512]{1,0:T(8,128)(2,1)S(1)}, u32[]{:S(2)}, u32[]{:S(2)}) collective-permute-start(bf16[1024,512]{1,0:T(8,128)(2,1)S(1)} %get-tuple-element.13), channel_id=1, source_target_pairs={{62,0},{63,1},{0,2},{1,3},{2,4},{3,5},{4,6},{5,7},{6,8},{7,9},{8,1... | collective-permute-start | bytes 3145736 | tf_op jit(solution)/shard_map/ppermute | solution.py:43
  55.0 28.9 %collective-permute-start.1 = (bf16[1024,512]{1,0:T(8,128)(2,1)S(1)}, bf16[1024,512]{1,0:T(8,128)(2,1)S(1)}, u32[]{:S(2)}, u32[]{:S(2)}) collective-permute-start(bf16[1024,512]{1,0:T(8,128)(2,1)S(1)} %get-tuple-element.13), channel_id=1, source_target_pairs={{2,0},{3,1},{4,2},{5,3},{6,4},{7,5},{8,6},{9,7},{10,8},{11,9},{12,... | collective-permute-start | bytes 3145736 | tf_op jit(solution)/shard_map/ppermute | solution.py:44
  61.4 26.5 %copy-start.6 = (bf16[256,1024]{1,0:T(8,128)(2,1)S(1)}, bf16[256,1024]{1,0:T(8,128)(2,1)}, u32[]{:S(2)}) copy-start(bf16[256,1024]{1,0:T(8,128)(2,1)} %get-tuple-element.3) | copy-start | bytes 1572868
  83.8 1.4 copy-start.2
  85.3 24.7 %collective-permute-start.2 = (bf16[1024,512]{1,0:T(8,128)(2,1)}, bf16[1024,512]{1,0:T(8,128)(2,1)S(1)}, u32[]{:S(2)}, u32[]{:S(2)}) collective-permute-start(bf16[1024,512]{1,0:T(8,128)(2,1)} %add_convert_fusion.4), channel_id=1, source_target_pairs={{1,0},{0,1},{3,2},{2,3},{5,4},{4,5},{7,6},{6,7},{9,8},{8,9},{11,10... | collective-permute-start | bytes 3145736 | tf_op jit(solution)/shard_map/ppermute | solution.py:48
  89.6 37.8 %all-to-all-start.1 = ((bf16[4,128,1536]{2,1,0:T(8,128)(2,1)}), bf16[4,128,1536]{2,1,0:T(8,128)(2,1)}, u32[]{:S(2)}, u32[]{:S(2)}) async-start(bf16[4,128,1536]{2,1,0:T(8,128)(2,1)} %bitcast.14), calls=%async_computation.1 | async-start | bytes 3145728 | tf_op jit(solution)/shard_map/all_to_all | solution.py:70
  110.0 1.0 copy-start.7
  127.4 2.2 copy-start.14
  129.7 4.1 %copy-start.10 = (bf16[512,512]{1,0:T(8,128)(2,1)}, bf16[512,512]{1,0:T(8,128)(2,1)S(1)}, u32[]{:S(2)}) copy-start(bf16[512,512]{1,0:T(8,128)(2,1)S(1)} %fusion.16) | copy-start | bytes 1572868
  154.0 33.9 %collective-permute-start.3 = (bf16[1024,512]{1,0:T(8,128)(2,1)}, bf16[1024,512]{1,0:T(8,128)(2,1)S(1)}, u32[]{:S(2)}, u32[]{:S(2)}) collective-permute-start(bf16[1024,512]{1,0:T(8,128)(2,1)} %get-tuple-element.17), channel_id=1, source_target_pairs={{62,0},{63,1},{0,2},{1,3},{2,4},{3,5},{4,6},{5,7},{6,8},{7,9},{8,1... | collective-permute-start | bytes 3145736 | tf_op jit(solution)/shard_map/ppermute | solution.py:43
  154.0 33.9 %collective-permute-start.4 = (bf16[1024,512]{1,0:T(8,128)(2,1)}, bf16[1024,512]{1,0:T(8,128)(2,1)}, u32[]{:S(2)}, u32[]{:S(2)}) collective-permute-start(bf16[1024,512]{1,0:T(8,128)(2,1)} %get-tuple-element.17), channel_id=1, source_target_pairs={{2,0},{3,1},{4,2},{5,3},{6,4},{7,5},{8,6},{9,7},{10,8},{11,9},{12,... | collective-permute-start | bytes 3145736 | tf_op jit(solution)/shard_map/ppermute | solution.py:44
  162.3 20.6 %all-to-all-start.2 = ((bf16[4,128,1024]{2,1,0:T(8,128)(2,1)}), bf16[4,128,1024]{2,1,0:T(8,128)(2,1)}, u32[]{:S(2)}, u32[]{:S(2)}) async-start(bf16[4,128,1024]{2,1,0:T(8,128)(2,1)} %bitcast.86), calls=%async_computation.2 | async-start | bytes 2097152 | tf_op jit(solution)/shard_map/all_to_all | solution.py:93
  171.9 16.1 %copy-start.5 = (bf16[1024,512]{1,0:T(8,128)(2,1)S(1)}, bf16[1024,512]{1,0:T(8,128)(2,1)}, u32[]{:S(2)}) copy-start(bf16[1024,512]{1,0:T(8,128)(2,1)} %get-tuple-element.17) | copy-start | bytes 3145732
  182.8 18.8 %all-to-all-start.3 = ((bf16[4,128,1024]{2,1,0:T(8,128)(2,1)}), bf16[4,128,1024]{2,1,0:T(8,128)(2,1)}, u32[]{:S(2)}, u32[]{:S(2)}) async-start(bf16[4,128,1024]{2,1,0:T(8,128)(2,1)} %bitcast.85), calls=%async_computation.3 | async-start | bytes 2097152 | tf_op jit(solution)/shard_map/all_to_all | solution.py:93
  187.9 3.0 %copy-start.3 = (bf16[1024,512]{1,0:T(8,128)(2,1)}, bf16[1024,512]{1,0:T(8,128)(2,1)S(1)}, u32[]{:S(2)}) copy-start(bf16[1024,512]{1,0:T(8,128)(2,1)S(1)} %collective-permute-done.3) | copy-start | bytes 3145732
  191.0 33.7 %collective-permute-start.5 = (bf16[1024,512]{1,0:T(8,128)(2,1)}, bf16[1024,512]{1,0:T(8,128)(2,1)}, u32[]{:S(2)}, u32[]{:S(2)}) collective-permute-start(bf16[1024,512]{1,0:T(8,128)(2,1)} %add_convert_fusion), channel_id=1, source_target_pairs={{1,0},{0,1},{3,2},{2,3},{5,4},{4,5},{7,6},{6,7},{9,8},{8,9},{11,10... | collective-permute-start | bytes 3145736 | tf_op jit(solution)/shard_map/ppermute | solution.py:48
  193.6 31.1 %copy-start.1 = (f32[1024,512]{1,0:T(8,128)S(1)}, f32[1024,512]{1,0:T(8,128)}, u32[]{:S(2)}) copy-start(f32[1024,512]{1,0:T(8,128)} %get-tuple-element.18) | copy-start | bytes 6291460
  193.6 31.1 %copy-start.4 = (bf16[1024,512]{1,0:T(8,128)(2,1)S(1)}, bf16[1024,512]{1,0:T(8,128)(2,1)}, u32[]{:S(2)}) copy-start(bf16[1024,512]{1,0:T(8,128)(2,1)} %copy-done.3) | copy-start | bytes 3145732

commit v2 on v1

v2 whole, which is shorter than its diff:
```python
import functools
import math

import jax
import jax.numpy as jnp
from jax import lax
from jax.experimental import pallas as pl
from jax.experimental.pallas import tpu as pltpu
from jax.sharding import PartitionSpec as P

ROUNDS = 2
NS_STEPS = 3
CHUNKS = 4
MESH = pl.DeviceIdType.MESH
F32 = jnp.float32
BF16 = jnp.bfloat16


def dot(a, b, ca=1, cb=0):
    return lax.dot_general(a, b, (((ca,), (cb,)), ((), ())), preferred_element_type=F32)


def kernel(
    nodes, experts,
    tok_hbm, route_ref, og_hbm, w_hbm, m_hbm,
    w_out, m_out, ig_out,
    tok, og, weight, moment, wide, table, sent, got, slope, orthog, gram, poly,
    back, ret, ig, shared, beside, pair, across,
    in_sem, out_sem, w_sem, d_send, d_recv, r_send, r_recv, z_send, z_recv, x_send, x_recv,
):
    expert = lax.axis_index("expert")
    node = lax.axis_index("node")
    rows, width = tok.shape[1], tok.shape[2]
    hidden = og.shape[2]
    cap = rows // 2
    tile = width // CHUNKS
    factor = 1.0 / math.sqrt(width)
    step_size = 0.1 * math.sqrt(width)

    chip, core = expert // 2, expert % 2
    mates = (
        expert,
        2 * chip + (1 - core),
        2 * (1 - chip) + core,
        2 * (1 - chip) + (1 - core),
    )
    odd = node % 2
    up = (node + 2) % nodes
    down = (node + nodes - 2) % nodes
    facing = node + 1 - 2 * odd

    loads = []
    for r in range(ROUNDS):
        loads.append(pltpu.make_async_copy(tok_hbm.at[r], tok.at[r], in_sem.at[2 * r]))
        loads.append(pltpu.make_async_copy(og_hbm.at[r], og.at[r], in_sem.at[2 * r + 1]))
    load_w = pltpu.make_async_copy(w_hbm.at[0, 0], weight, in_sem.at[4])
    load_m = pltpu.make_async_copy(m_hbm.at[0, 0], moment, in_sem.at[5])
    for copy in (loads[0], loads[1], load_w, load_m, loads[2], loads[3]):
        copy.start()

    barrier = pltpu.get_barrier_semaphore()
    for mate in mates[1:]:
        pl.semaphore_signal(barrier, inc=1, device_id=(mate, node), device_id_type=MESH)
    for other in (up, down, facing):
        pl.semaphore_signal(barrier, inc=1, device_id=(expert, other), device_id_type=MESH)

    def block(index):
        return pl.ds(pl.multiple_of(index * cap, cap), cap)

    def fixed(index):
        return pl.ds(index * cap, cap)

    def strip(index):
        return pl.ds(pl.multiple_of(index * tile, tile), tile)

    def dispatch(r):
        route = route_ref[r : r + 1, :]
        mask = lax.broadcasted_iota(jnp.int32, (16, rows), 0) == route
        first = lax.broadcasted_iota(jnp.int32, (rows, rows), 0)
        second = lax.broadcasted_iota(jnp.int32, (rows, rows), 1)
        earlier = jnp.where(first < second, 1.0, 0.0).astype(BF16)
        ranks = dot(jnp.where(mask, 1.0, 0.0).astype(BF16), earlier)
        rank = jnp.sum(jnp.where(mask, ranks, 0.0), axis=0, keepdims=True)
        target = route.astype(F32) * float(cap) + rank
        for e in range(experts):
            slots = (lax.broadcasted_iota(jnp.int32, (cap, rows), 0) + e * cap).astype(F32)
            picks = jnp.where(slots == target, 1.0, 0.0).astype(BF16)
            table[r, fixed(e), :] = picks
            sent[r, fixed(e), :width] = dot(picks, tok[r]).astype(BF16)
            sent[r, fixed(e), width:] = dot(picks, og[r]).astype(BF16)

    def dispatch_copy(r, k):
        return pltpu.make_async_remote_copy(
            src_ref=sent.at[r, block(mates[k])],
            dst_ref=got.at[r, fixed(k)],
            send_sem=d_send.at[r, k],
            recv_sem=d_recv.at[r, k],
            device_id=(mates[k], node),
            device_id_type=MESH,
        )

    def return_copy(r, k):
        return pltpu.make_async_remote_copy(
            src_ref=back.at[r, fixed(k)],
            dst_ref=ret.at[r, block(expert)],
            send_sem=r_send.at[r, k],
            recv_sem=r_recv.at[r, k],
            device_id=(mates[k], node),
            device_id_type=MESH,
        )

    def z_copy(r, way, j):
        return pltpu.make_async_remote_copy(
            src_ref=shared.at[r, strip(j)],
            dst_ref=beside.at[r, way, strip(j)],
            send_sem=z_send.at[r, way, j],
            recv_sem=z_recv.at[r, way, j],
            device_id=(expert, down if way else up),
            device_id_type=MESH,
        )

    def x_copy(r, j):
        return pltpu.make_async_remote_copy(
            src_ref=pair.at[r, strip(j)],
            dst_ref=across.at[r, strip(j)],
            send_sem=x_send.at[r, j],
            recv_sem=x_recv.at[r, j],
            device_id=(expert, facing),
            device_id_type=MESH,
        )

    def start_dispatch(r):
        for k in (2, 3, 1):
            dispatch_copy(r, k).start()
        got[r, fixed(0), :] = sent[r, block(expert), :]

    def start_return(r):
        for k in (2, 3, 1):
            return_copy(r, k).start()
        ret[r, block(expert), :] = back[r, fixed(0), :]

    def slopes(r, half):
        part = pl.ds(half * rows, rows)
        pre = dot(got[r, part, :width], wide[...]) * factor
        grads = got[r, part, width:].astype(F32)
        slope[part, :] = (grads * 2.0 * jnp.maximum(pre, 0.0)).astype(BF16)

    def update_moment(r):
        def body(j, total):
            columns = pl.ds(pl.multiple_of(j * tile, tile), tile)
            grad = dot(got[r, :, columns], slope[...], 0, 0) * factor
            new = 0.9 * moment[strip(j), :] + grad
            moment[strip(j), :] = new
            return total + jnp.sum(new * new, axis=0, keepdims=True)

        total = lax.fori_loop(0, CHUNKS, body, jnp.zeros((1, hidden), F32))
        norm = jnp.sqrt(jnp.sum(total, axis=1, keepdims=True))
        scale = 1.0 / (norm + 1e-07)

        def scaled(j, carry):
            orthog[strip(j), :] = (moment[strip(j), :] * scale).astype(BF16)
            return carry

        lax.fori_loop(0, CHUNKS, scaled, 0)

    def polynomial():
        part = hidden // 2
        for i in range(2):
            columns = pl.ds(i * part, part)
            gram[columns, :] = dot(orthog[:, columns], orthog[...], 0, 0).astype(BF16)
        for i in range(2):
            columns = pl.ds(i * part, part)
            own = gram[columns, :]
            square = dot(own, gram[...])
            poly[columns, :] = (-4.775 * own.astype(F32) + 2.0315 * square).astype(BF16)

    def applied(j):
        own = orthog[strip(j), :]
        return (3.4445 * own.astype(F32) + dot(own, poly[...])).astype(BF16)

    def orthogonalize_and_share(r):
        def sweep(i, carry):
            polynomial()

            def body(j, inner):
                orthog[strip(j), :] = applied(j)
                return inner

            return lax.fori_loop(0, CHUNKS, body, carry)

        lax.fori_loop(0, NS_STEPS - 1, sweep, 0)
        polynomial()

        def last(j, carry):
            stepped = weight[strip(j), :] - step_size * applied(j).astype(F32)
            weight[strip(j), :] = stepped
            shared[r, strip(j), :] = stepped.astype(BF16)
            z_copy(r, 0, j).start()
            z_copy(r, 1, j).start()
            return carry

        lax.fori_loop(0, CHUNKS, last, 0)

    def backward(r):
        for half in range(2):
            part = pl.ds(half * rows, rows)

            def body(j, carry, part=part):
                columns = pl.ds(pl.multiple_of(j * tile, tile), tile)
                grad = dot(slope[part, :], wide[strip(j), :], 1, 1) * factor
                back[r, part, columns] = grad.astype(BF16)
                return carry

            lax.fori_loop(0, CHUNKS, body, 0)

    def unsort(r):
        for k in (1, 2, 3):
            return_copy(r, k).wait_recv()

        def body(j, carry):
            columns = pl.ds(pl.multiple_of(j * tile, tile), tile)
            ig[r, :, columns] = dot(table[r], ret[r, :, columns], 0, 0).astype(BF16)
            return carry

        lax.fori_loop(0, CHUNKS, body, 0)
        pltpu.make_async_copy(ig.at[r], ig_out.at[r], out_sem.at[r]).start()

    def pass_across(r):
        def body(j, carry):
            z_copy(r, 0, j).wait_recv()
            z_copy(r, 1, j).wait_recv()
            own = shared[r, strip(j), :].astype(F32)
            pair[r, strip(j), :] = (own + beside[r, 1 - odd, strip(j), :].astype(F32)).astype(BF16)
            x_copy(r, j).start()
            return carry

        lax.fori_loop(0, CHUNKS, body, 0)

    def averaged(r, j):
        x_copy(r, j).wait_recv()
        neighbours = beside[r, 0, strip(j), :].astype(F32) + beside[r, 1, strip(j), :].astype(F32)
        neighbours = neighbours + across[r, strip(j), :].astype(F32)
        new = 0.4 * weight[strip(j), :] + 0.15 * neighbours
        weight[strip(j), :] = new
        return new

    loads[0].wait()
    loads[1].wait()
    dispatch(0)
    pl.semaphore_wait(barrier, 6)
    start_dispatch(0)
    loads[2].wait()
    loads[3].wait()
    dispatch(1)
    load_w.wait()

    def narrow(j, carry):
        wide[strip(j), :] = weight[strip(j), :].astype(BF16)
        return carry

    lax.fori_loop(0, CHUNKS, narrow, 0)
    load_m.wait()
    dispatch_copy(0, 1).wait_recv()
    slopes(0, 0)
    dispatch_copy(0, 2).wait_recv()
    dispatch_copy(0, 3).wait_recv()
    start_dispatch(1)
    slopes(0, 1)
    update_moment(0)
    orthogonalize_and_share(0)
    backward(0)
    pass_across(0)

    def mixed(j, carry):
        wide[strip(j), :] = averaged(0, j).astype(BF16)
        return carry

    lax.fori_loop(0, CHUNKS, mixed, 0)

    start_return(0)
    for k in (1, 2, 3):
        dispatch_copy(1, k).wait_recv()
    slopes(1, 0)
    slopes(1, 1)
    update_moment(1)
    give_m = pltpu.make_async_copy(moment, m_out.at[0, 0], out_sem.at[2])
    give_m.start()
    orthogonalize_and_share(1)
    backward(1)
    start_return(1)
    pass_across(1)
    unsort(0)

    def finished(j, carry):
        averaged(1, j)
        pltpu.make_async_copy(weight.at[strip(j)], w_out.at[0, 0, strip(j)], w_sem.at[j]).start()
        return carry

    lax.fori_loop(0, CHUNKS, finished, 0)
    unsort(1)

    for r in range(ROUNDS):
        for k in (1, 2, 3):
            dispatch_copy(r, k).wait_send()
            return_copy(r, k).wait_send()

        def sent_all(j, carry, r=r):
            z_copy(r, 0, j).wait_send()
            z_copy(r, 1, j).wait_send()
            x_copy(r, j).wait_send()
            return carry

        lax.fori_loop(0, CHUNKS, sent_all, 0)
        pltpu.make_async_copy(ig.at[r], ig_out.at[r], out_sem.at[r]).wait()
    give_m.wait()

    def given(j, carry):
        pltpu.make_async_copy(weight.at[strip(j)], w_out.at[0, 0, strip(j)], w_sem.at[j]).wait()
        return carry

    lax.fori_loop(0, CHUNKS, given, 0)


def on_device(tokens, routing, out_grad, weights, momentum):
    rounds, rows, width = tokens.shape
    hidden = out_grad.shape[2]
    experts = weights.shape[1] * lax.axis_size("expert")
    nodes = lax.axis_size("node")
    slots = experts * (rows // 2)
    anywhere = pl.BlockSpec(memory_space=pl.ANY)
    dma = pltpu.SemaphoreType.DMA
    return pl.pallas_call(
        functools.partial(kernel, nodes, experts),
        name="muon_rounds",
        out_shape=(
            jax.ShapeDtypeStruct(weights.shape, F32),
            jax.ShapeDtypeStruct(momentum.shape, F32),
            jax.ShapeDtypeStruct(tokens.shape, BF16),
        ),
        in_specs=[anywhere, pl.BlockSpec(memory_space=pltpu.VMEM), anywhere, anywhere, anywhere],
        out_specs=(anywhere, anywhere, anywhere),
        scratch_shapes=[
            pltpu.VMEM((rounds, rows, width), BF16),
            pltpu.VMEM((rounds, rows, hidden), BF16),
            pltpu.VMEM((width, hidden), F32),
            pltpu.VMEM((width, hidden), F32),
            pltpu.VMEM((width, hidden), BF16),
            pltpu.VMEM((rounds, slots, rows), BF16),
            pltpu.VMEM((rounds, slots, width + hidden), BF16),
            pltpu.VMEM((rounds, slots, width + hidden), BF16),
            pltpu.VMEM((slots, hidden), BF16),
            pltpu.VMEM((width, hidden), BF16),
            pltpu.VMEM((hidden, hidden), BF16),
            pltpu.VMEM((hidden, hidden), BF16),
            pltpu.VMEM((rounds, slots, width), BF16),
            pltpu.VMEM((rounds, slots, width), BF16),
            pltpu.VMEM((rounds, rows, width), BF16),
            pltpu.VMEM((rounds, width, hidden), BF16),
            pltpu.VMEM((rounds, 2, width, hidden), BF16),
            pltpu.VMEM((rounds, width, hidden), BF16),
            pltpu.VMEM((rounds, width, hidden), BF16),
            dma((6,)),
            dma((3,)),
            dma((CHUNKS,)),
            dma((rounds, 4)),
            dma((rounds, 4)),
            dma((rounds, 4)),
            dma((rounds, 4)),
            dma((rounds, 2, CHUNKS)),
            dma((rounds, 2, CHUNKS)),
            dma((rounds, CHUNKS)),
            dma((rounds, CHUNKS)),
        ],
        compiler_params=pltpu.CompilerParams(
            collective_id=0, has_side_effects=True, vmem_limit_bytes=56 << 20
        ),
    )(tokens, routing, out_grad, weights, momentum)


def solution(mesh):
    return jax.shard_map(
        on_device,
        mesh=mesh,
        in_specs=(
            P(None, ("expert", "node"), None),
            P(None, ("expert", "node")),
            P(None, ("expert", "node"), None),
            P("node", "expert", None, None),
            P("node", "expert", None, None),
        ),
        out_specs=(
            P("node", "expert", None, None),
            P("node", "expert", None, None),
            P(None, ("expert", "node"), None),
        ),
        check_vma=False,
    )
```

time: 229 us -> 128 us (0.56)
  Pallas kernels: 0 us -> 121 us
  waiting for transfers between devices: 88.4 us -> 0 us
  matrix products: 61 us -> 0 us
  starting transfers between devices: 32.1 us -> 0 us
  blocking collectives: 24.9 us -> 0 us
  other arithmetic: 12.8 us -> 0 us
    pallas_call x0 -> x1, Pallas kernels: none -> 121 us  [on_device(): pl.pallas_call(functools.partial(kernel, nodes, experts), name='muon_roun...]
    dot_general x24 -> x0, matrix products: 61 us -> none  [the longest x6 23.4 us: orthogonalize(): jnp.dot(orthog, polynom, preferred_element_type=jnp.float32)]
    ppermute x6 -> x0, waiting for transfers between devices: 55.8 us -> none  [the longest x2 33.3 us: neighbour_sum(): across = lax.ppermute(pair, 'node', [(i ^ 1, i) for i in range(nodes)])]
    all_to_all x3 -> x0, waiting for transfers between devices: 32.6 us -> none  [the longest x2 19 us: on_device(): lax.all_to_all(backward, 'expert', split_axis=0, concat_axis=0, tiled=True)]
    all_to_all x1 -> x0, blocking collectives: 24.9 us -> none  [on_device(): lax.all_to_all(sent, 'expert', split_axis=0, concat_axis=0, tiled=True)]
    all_to_all x3 -> x0, starting transfers between devices: 18.2 us -> none  [the longest x2 12 us: on_device(): lax.all_to_all(backward, 'expert', split_axis=0, concat_axis=0, tiled=True)]
    ppermute x6 -> x0, starting transfers between devices: 13.9 us -> none  [the longest x2 11.2 us: neighbour_sum(): lax.ppermute(shared, 'node', [((i + 2) % nodes, i) for i in range(nodes)])]
    convert_element_type x4 -> x0, other arithmetic: 4.43 us -> none  [the longest x2 4.42 us: neighbour_sum(): (shared.astype(jnp.float32) + beside.astype(jnp.float32)).astype(jnp.bflo...]
  transfers between devices with their start and end apart: 9 -> 0, of which waited for: 6 -> 0; matrix products, arithmetic and copies ran while one was open for 9% -> 0% of each run, Pallas kernels for 0% -> 0%
where the time goes in v2:
time: 128 us
  Pallas kernels  121 us (95%)
  local copies, waits for them, and re-layouts  6.16 us (5%)
    pallas_call x1, Pallas kernels, on_device(): pl.pallas_call(functools.partial(kernel, nodes, experts), name='muon_roun...  121 us
    unnamed x7, local copies, waits for them, and re-layouts  6.16 us

profile of v2, /device:TPU:1, one launch (start us, length us, event | category | flops | bytes accessed | tf_op | source)
XLA Modules:
  0.0 128.0 jit_solution(218003523925930724)
XLA Ops:
  0.6 121.2 %muon_rounds.1 = (f32[1,1,1024,512]{3,2,1,0:T(8,128)}, f32[1,1,1024,512]{3,2,1,0:T(8,128)}, bf16[2,256,1024]{2,1,0:T(8,128)(2,1)}) custom-call(bf16[2,256,1024]{2,1,0:T(8,128)(2,1)} %tok_hbm.1, s32[2,256]{1,0:T(2,128)} %route_ref.1, bf16[2,256,512]{2,1,0:T(8,128)(2,1)} %og_hbm.1, f32[1,1,1024,512]{3,2,1,0:T(8,128)} %w_hbm.1, f32[1,1,1024,512]{3,2,1,0:T(8,128)} %m_hbm.1), custom_call_target="tpu_custom_call" | custom-call | tf_op jit(solution)/shard_map/muon_rounds/pallas_call | solution.py:332
  121.8 0.0 copy-start
  121.8 3.2 %copy.11 = f32[1,1,1024,512]{3,2,1,0:T(8,128)} copy(f32[1,1,1024,512]{3,2,1,0:T(8,128)} %get-tuple-element.6) | data formatting | bytes 4194304
  125.1 0.0 copy-done
  125.1 0.0 copy-start.1
  125.1 1.3 %copy.12 = f32[1,1,1024,512]{3,2,1,0:T(8,128)} copy(f32[1,1,1024,512]{3,2,1,0:T(8,128)S(1)} %copy-done) | data formatting | bytes 4194304
  126.4 0.6 copy-done.1
  127.0 1.0 copy.13
Async XLA Ops:
  121.8 3.2 %copy-start = (f32[1,1,1024,512]{3,2,1,0:T(8,128)S(1)}, f32[1,1,1024,512]{3,2,1,0:T(8,128)}, u32[]{:S(2)}) copy-start(f32[1,1,1024,512]{3,2,1,0:T(8,128)} %get-tuple-element.7) | copy-start | bytes 6291460
  125.1 2.0 %copy-start.1 = (bf16[2,256,1024]{2,1,0:T(8,128)(2,1)S(1)}, bf16[2,256,1024]{2,1,0:T(8,128)(2,1)}, u32[]{:S(2)}) copy-start(bf16[2,256,1024]{2,1,0:T(8,128)(2,1)} %get-tuple-element.8) | copy-start | bytes 3145732

commit v3 on v2

v3 whole, which is shorter than its diff:
```python
import functools
import math

import jax
import jax.numpy as jnp
from jax import lax
from jax.experimental import pallas as pl
from jax.experimental.pallas import tpu as pltpu
from jax.sharding import PartitionSpec as P

ROUNDS = 2
NS_STEPS = 3
CHUNKS = 4
PIECES = 8
MESH = pl.DeviceIdType.MESH
F32 = jnp.float32
BF16 = jnp.bfloat16


def dot(a, b, ca=1, cb=0):
    return lax.dot_general(a, b, (((ca,), (cb,)), ((), ())), preferred_element_type=F32)


def kernel(
    nodes,
    tok_hbm, route_hbm, og_hbm, w_hbm, m_hbm,
    weight, moment, ig,
    route_ref, tok, og, wide, table, sent, got, slope, orthog, gram, poly,
    back, ret, shared, beside, pair, across,
    in_sem, d_send, d_recv, r_send, r_recv, z_send, z_recv, x_send, x_recv,
):
    expert = lax.axis_index("expert")
    node = lax.axis_index("node")
    rows, width = tok.shape[1], tok.shape[2]
    hidden = og.shape[2]
    cap = rows // 2
    tile = width // CHUNKS
    piece = width // PIECES
    factor = 1.0 / math.sqrt(width)
    step_size = 0.1 * math.sqrt(width)

    chip, core = expert // 2, expert % 2
    mates = (
        expert,
        2 * chip + (1 - core),
        2 * (1 - chip) + core,
        2 * (1 - chip) + (1 - core),
    )
    odd = node % 2
    up = (node + 2) % nodes
    down = (node + nodes - 2) % nodes
    facing = node + 1 - 2 * odd

    loads = []
    for r in range(ROUNDS):
        loads.append(pltpu.make_async_copy(tok_hbm.at[r], tok.at[r], in_sem.at[2 * r]))
        loads.append(pltpu.make_async_copy(og_hbm.at[r], og.at[r], in_sem.at[2 * r + 1]))
    load_w = pltpu.make_async_copy(w_hbm.at[0, 0], weight, in_sem.at[4])
    load_route = pltpu.make_async_copy(route_hbm, route_ref, in_sem.at[6])
    load_m = pltpu.make_async_copy(m_hbm.at[0, 0], moment, in_sem.at[5])
    for copy in (load_route, *loads[:2]):
        copy.start()

    barrier = pltpu.get_barrier_semaphore()
    for mate in mates[1:]:
        pl.semaphore_signal(barrier, inc=1, device_id=(mate, node), device_id_type=MESH)
    for other in (up, down, facing):
        pl.semaphore_signal(barrier, inc=1, device_id=(expert, other), device_id_type=MESH)

    def fixed(index):
        return pl.ds(index * cap, cap)

    def strip(index):
        return pl.ds(pl.multiple_of(index * tile, tile), tile)

    def bit(index):
        return pl.ds(pl.multiple_of(index * piece, piece), piece)

    def targets(r):
        route = route_ref[r : r + 1, :]
        mask = lax.broadcasted_iota(jnp.int32, (16, rows), 0) == route
        first = lax.broadcasted_iota(jnp.int32, (rows, rows), 0)
        second = lax.broadcasted_iota(jnp.int32, (rows, rows), 1)
        earlier = jnp.where(first < second, 1.0, 0.0).astype(BF16)
        ranks = dot(jnp.where(mask, 1.0, 0.0).astype(BF16), earlier)
        rank = jnp.sum(jnp.where(mask, ranks, 0.0), axis=0, keepdims=True)
        return route.astype(F32) * float(cap) + rank

    def choose(r, k, target):
        slots = lax.broadcasted_iota(jnp.int32, (cap, rows), 0) + mates[k] * cap
        picks = jnp.where(slots.astype(F32) == target, 1.0, 0.0).astype(BF16)
        table[r, fixed(k), :] = picks
        held = sent if k else got
        held[r, fixed(k), :width] = dot(picks, tok[r]).astype(BF16)
        held[r, fixed(k), width:] = dot(picks, og[r]).astype(BF16)

    def dispatch_copy(r, k):
        return pltpu.make_async_remote_copy(
            src_ref=sent.at[r, fixed(k)],
            dst_ref=got.at[r, fixed(k)],
            send_sem=d_send.at[r, k],
            recv_sem=d_recv.at[r, k],
            device_id=(mates[k], node),
            device_id_type=MESH,
        )

    def return_copy(r, k):
        return pltpu.make_async_remote_copy(
            src_ref=back.at[r, fixed(k)],
            dst_ref=ret.at[r, fixed(k)],
            send_sem=r_send.at[r, k],
            recv_sem=r_recv.at[r, k],
            device_id=(mates[k], node),
            device_id_type=MESH,
        )

    def z_copy(r, way, j):
        return pltpu.make_async_remote_copy(
            src_ref=shared.at[r, bit(j)],
            dst_ref=beside.at[r, way, bit(j)],
            send_sem=z_send.at[r, way, j],
            recv_sem=z_recv.at[r, way, j],
            device_id=(expert, way * down + (1 - way) * up),
            device_id_type=MESH,
        )

    def x_copy(r, j):
        return pltpu.make_async_remote_copy(
            src_ref=pair.at[r, bit(j)],
            dst_ref=across.at[r, bit(j)],
            send_sem=x_send.at[r, j],
            recv_sem=x_recv.at[r, j],
            device_id=(expert, facing),
            device_id_type=MESH,
        )

    def start_return(r):
        for k in (2, 3, 1):
            return_copy(r, k).start()

    def slopes(r, half):
        part = pl.ds(half * rows, rows)
        pre = dot(got[r, part, :width], wide[...]) * factor
        grads = got[r, part, width:].astype(F32)
        slope[part, :] = (grads * 2.0 * jnp.maximum(pre, 0.0)).astype(BF16)

    def update_moment(r):
        def body(j, total):
            columns = pl.ds(pl.multiple_of(j * tile, tile), tile)
            grad = dot(got[r, :, columns], slope[...], 0, 0) * factor
            new = 0.9 * moment[strip(j), :] + grad
            moment[strip(j), :] = new
            return total + jnp.sum(new * new, axis=0, keepdims=True)

        total = lax.fori_loop(0, CHUNKS, body, jnp.zeros((1, hidden), F32))
        norm = jnp.sqrt(jnp.sum(total, axis=1, keepdims=True))
        scale = 1.0 / (norm + 1e-07)

        def scaled(j, carry):
            orthog[strip(j), :] = (moment[strip(j), :] * scale).astype(BF16)
            return carry

        lax.fori_loop(0, CHUNKS, scaled, 0)

    def polynomial():
        part = hidden // 2
        for i in range(2):
            columns = pl.ds(i * part, part)
            gram[columns, :] = dot(orthog[:, columns], orthog[...], 0, 0).astype(BF16)
        for i in range(2):
            columns = pl.ds(i * part, part)
            own = gram[columns, :]
            square = dot(own, gram[...])
            poly[columns, :] = (-4.775 * own.astype(F32) + 2.0315 * square).astype(BF16)

    def applied(j):
        own = orthog[strip(j), :]
        return (3.4445 * own.astype(F32) + dot(own, poly[...])).astype(BF16)

    def orthogonalize_and_share(r):
        def sweep(i, carry):
            polynomial()

            def body(j, inner):
                orthog[strip(j), :] = applied(j)
                return inner

            return lax.fori_loop(0, CHUNKS, body, carry)

        lax.fori_loop(0, NS_STEPS - 1, sweep, 0)
        polynomial()

        def last(j, carry):
            stepped = weight[strip(j), :] - step_size * applied(j).astype(F32)
            weight[strip(j), :] = stepped
            shared[r, strip(j), :] = stepped.astype(BF16)
            for i in range(PIECES // CHUNKS):
                z_copy(r, 0, j * (PIECES // CHUNKS) + i).start()
                z_copy(r, 1, j * (PIECES // CHUNKS) + i).start()
            return carry

        lax.fori_loop(0, CHUNKS, last, 0)

    def backward(r):
        for half in (1, 0):
            part = pl.ds(half * rows, rows)

            def body(j, carry, part=part):
                columns = pl.ds(pl.multiple_of(j * tile, tile), tile)
                grad = dot(slope[part, :], wide[strip(j), :], 1, 1) * factor
                back[r, part, columns] = grad.astype(BF16)
                return carry

            lax.fori_loop(0, CHUNKS, body, 0)
        ret[r, fixed(0), :] = back[r, fixed(0), :]

    def unsort(r):
        for k in (1, 2, 3):
            return_copy(r, k).wait_recv()

        def body(j, carry):
            columns = pl.ds(pl.multiple_of(j * tile, tile), tile)
            ig[r, :, columns] = dot(table[r], ret[r, :, columns], 0, 0).astype(BF16)
            return carry

        lax.fori_loop(0, CHUNKS, body, 0)

    def pass_across(r):
        def body(j, carry):
            z_copy(r, 1 - odd, j).wait_recv()
            own = shared[r, bit(j), :].astype(F32)
            pair[r, bit(j), :] = (own + beside[r, 1 - odd, bit(j), :].astype(F32)).astype(BF16)
            x_copy(r, j).start()
            return carry

        lax.fori_loop(0, PIECES, body, 0)

    def averaged(r, j):
        z_copy(r, odd, j).wait_recv()
        x_copy(r, j).wait_recv()
        neighbours = beside[r, 0, bit(j), :].astype(F32) + beside[r, 1, bit(j), :].astype(F32)
        neighbours = neighbours + across[r, bit(j), :].astype(F32)
        new = 0.4 * weight[bit(j), :] + 0.15 * neighbours
        weight[bit(j), :] = new
        return new

    load_route.wait()
    target = targets(0)
    loads[0].wait()
    loads[1].wait()
    for copy in (loads[2], loads[3], load_w, load_m):
        copy.start()
    choose(0, 2, target)
    pl.semaphore_wait(barrier, 6)
    dispatch_copy(0, 2).start()
    for k in (3, 1):
        choose(0, k, target)
        dispatch_copy(0, k).start()
    choose(0, 0, target)
    target = targets(1)
    loads[2].wait()
    loads[3].wait()
    for k in (2, 3, 1):
        choose(1, k, target)
        dispatch_copy(1, k).start()
    choose(1, 0, target)
    load_w.wait()

    def narrow(j, carry):
        wide[strip(j), :] = weight[strip(j), :].astype(BF16)
        return carry

    lax.fori_loop(0, CHUNKS, narrow, 0)
    load_m.wait()
    dispatch_copy(0, 1).wait_recv()
    slopes(0, 0)
    dispatch_copy(0, 2).wait_recv()
    dispatch_copy(0, 3).wait_recv()
    slopes(0, 1)
    update_moment(0)
    orthogonalize_and_share(0)
    backward(0)
    pass_across(0)
    start_return(0)

    def mixed(j, carry):
        wide[bit(j), :] = averaged(0, j).astype(BF16)
        return carry

    lax.fori_loop(0, PIECES, mixed, 0)

    for k in (1, 2, 3):
        dispatch_copy(1, k).wait_recv()
    slopes(1, 0)
    slopes(1, 1)
    backward(1)
    start_return(1)
    update_moment(1)
    orthogonalize_and_share(1)
    unsort(0)
    pass_across(1)
    unsort(1)

    def finished(j, carry):
        averaged(1, j)
        return carry

    lax.fori_loop(0, PIECES, finished, 0)

    for r in range(ROUNDS):
        for k in (1, 2, 3):
            dispatch_copy(r, k).wait_send()
            return_copy(r, k).wait_send()

        def sent_all(j, carry, r=r):
            z_copy(r, 0, j).wait_send()
            z_copy(r, 1, j).wait_send()
            x_copy(r, j).wait_send()
            return carry

        lax.fori_loop(0, PIECES, sent_all, 0)


def store(weight, moment, ig, w_out, m_out, ig_out, sems):
    copies = (
        pltpu.make_async_copy(weight, w_out.at[0, 0], sems.at[0]),
        pltpu.make_async_copy(moment, m_out.at[0, 0], sems.at[1]),
        pltpu.make_async_copy(ig, ig_out, sems.at[2]),
    )
    for copy in copies:
        copy.start()
    for copy in copies:
        copy.wait()


def on_device(tokens, routing, out_grad, weights, momentum):
    rounds, rows, width = tokens.shape
    hidden = out_grad.shape[2]
    experts = weights.shape[1] * lax.axis_size("expert")
    nodes = lax.axis_size("node")
    slots = experts * (rows // 2)
    anywhere = pl.BlockSpec(memory_space=pl.ANY)
    in_hbm = pl.BlockSpec(memory_space=pltpu.HBM)
    on_chip = pl.BlockSpec(memory_space=pltpu.VMEM)
    dma = pltpu.SemaphoreType.DMA
    operands = (
        pltpu.with_memory_space_constraint(x, pltpu.HBM)
        for x in (tokens, routing, out_grad, weights, momentum)
    )
    weight, moment, in_grad = pl.pallas_call(
        functools.partial(kernel, nodes),
        name="muon_rounds",
        out_shape=(
            pltpu.VMEM((width, hidden), F32),
            pltpu.VMEM((width, hidden), F32),
            pltpu.VMEM((rounds, rows, width), BF16),
        ),
        in_specs=[in_hbm] * 5,
        out_specs=(on_chip, on_chip, on_chip),
        scratch_shapes=[
            pltpu.VMEM((rounds, rows), jnp.int32),
            pltpu.VMEM((rounds, rows, width), BF16),
            pltpu.VMEM((rounds, rows, hidden), BF16),
            pltpu.VMEM((width, hidden), BF16),
            pltpu.VMEM((rounds, slots, rows), BF16),
            pltpu.VMEM((rounds, slots, width + hidden), BF16),
            pltpu.VMEM((rounds, slots, width + hidden), BF16),
            pltpu.VMEM((slots, hidden), BF16),
            pltpu.VMEM((width, hidden), BF16),
            pltpu.VMEM((hidden, hidden), BF16),
            pltpu.VMEM((hidden, hidden), BF16),
            pltpu.VMEM((rounds, slots, width), BF16),
            pltpu.VMEM((rounds, slots, width), BF16),
            pltpu.VMEM((rounds, width, hidden), BF16),
            pltpu.VMEM((rounds, 2, width, hidden), BF16),
            pltpu.VMEM((rounds, width, hidden), BF16),
            pltpu.VMEM((rounds, width, hidden), BF16),
            dma((7,)),
            dma((rounds, 4)),
            dma((rounds, 4)),
            dma((rounds, 4)),
            dma((rounds, 4)),
            dma((rounds, 2, PIECES)),
            dma((rounds, 2, PIECES)),
            dma((rounds, PIECES)),
            dma((rounds, PIECES)),
        ],
        compiler_params=pltpu.CompilerParams(
            collective_id=0, has_side_effects=True, vmem_limit_bytes=40 << 20
        ),
    )(*operands)
    return pl.pallas_call(
        store,
        name="store_results",
        out_shape=(
            jax.ShapeDtypeStruct(weights.shape, F32),
            jax.ShapeDtypeStruct(momentum.shape, F32),
            jax.ShapeDtypeStruct(tokens.shape, BF16),
        ),
        in_specs=[anywhere, anywhere, anywhere],
        out_specs=(anywhere, anywhere, anywhere),
        scratch_shapes=[dma((3,))],
        compiler_params=pltpu.CompilerParams(vmem_limit_bytes=1 << 20),
    )(weight, moment, in_grad)


def solution(mesh):
    return jax.shard_map(
        on_device,
        mesh=mesh,
        in_specs=(
            P(None, ("expert", "node"), None),
            P(None, ("expert", "node")),
            P(None, ("expert", "node"), None),
            P("node", "expert", None, None),
            P("node", "expert", None, None),
        ),
        out_specs=(
            P("node", "expert", None, None),
            P("node", "expert", None, None),
            P(None, ("expert", "node"), None),
        ),
        check_vma=False,
    )
```

time: 128 us -> 118 us (0.922)
  local copies, waits for them, and re-layouts: 6.16 us -> 0 us
  Pallas kernels: 121 us -> 118 us
    unnamed x7 -> x0, local copies, waits for them, and re-layouts: 6.16 us -> none
    pallas_call x1 -> x2, Pallas kernels: 121 us -> 118 us  [the longest x1 115 us: on_device(): pl.pallas_call(functools.partial(kernel, nodes), name='muon_rounds', out_...]
where the time goes in v3:
time: 118 us
  Pallas kernels  118 us (100%)
    pallas_call x1, Pallas kernels, on_device(): pl.pallas_call(functools.partial(kernel, nodes), name='muon_rounds', out_...  115 us
    pallas_call x1, Pallas kernels, on_device(): pl.pallas_call(store, name='store_results', out_shape=(jax.ShapeDtypeStru...  2.38 us

profile of v3, /device:TPU:1, one launch (start us, length us, event | category | flops | bytes accessed | tf_op | source)
XLA Modules:
  0.0 118.2 jit_solution(12121051263328794829)
XLA Ops:
  0.6 115.2 %muon_rounds.1 = (f32[1024,512]{1,0:T(8,128)S(1)}, f32[1024,512]{1,0:T(8,128)S(1)}, bf16[2,256,1024]{2,1,0:T(8,128)(2,1)S(1)}) custom-call(bf16[2,256,1024]{2,1,0:T(8,128)(2,1)} %tok_hbm.1, s32[2,256]{1,0:T(2,128)} %route_hbm.1, bf16[2,256,512]{2,1,0:T(8,128)(2,1)} %og_hbm.1, f32[1,1,1024,512]{3,2,1,0:T(8,128)} %w_hbm.1, f32[1,1,1024,512]{3,2,1,0:T(8,128)} %m_hbm.1), custom_call_target="tpu_custom_call" | custom-call | tf_op jit(solution)/shard_map/muon_rounds/pallas_call | solution.py:350
  115.8 2.4 %store_results.1 = (f32[1,1,1024,512]{3,2,1,0:T(8,128)}, f32[1,1,1024,512]{3,2,1,0:T(8,128)}, bf16[2,256,1024]{2,1,0:T(8,128)(2,1)}) custom-call(f32[1024,512]{1,0:T(8,128)S(1)} %get-tuple-element.6.weight, f32[1024,512]{1,0:T(8,128)S(1)} %get-tuple-element.7.moment, bf16[2,256,1024]{2,1,0:T(8,128)(2,1)S(1)} %get-tuple-element.8.ig), custom_call_target="tpu_custom_call" | custom-call | tf_op jit(solution)/shard_map/store_results/pallas_call | solution.py:392

commit v4 on v3

--- a/solution.py
+++ b/solution.py
@@ -27,7 +27,7 @@
     weight, moment, ig,
     route_ref, tok, og, wide, table, sent, got, slope, orthog, gram, poly,
     back, ret, shared, beside, pair, across,
-    in_sem, d_send, d_recv, r_send, r_recv, z_send, z_recv, x_send, x_recv,
+    in_sem, d_send, d_recv, r_send, r_recv, z_send, z_recv, x_send, x_recv, ready,
 ):
     expert = lax.axis_index("expert")
     node = lax.axis_index("node")
@@ -64,8 +64,17 @@
     barrier = pltpu.get_barrier_semaphore()
     for mate in mates[1:]:
         pl.semaphore_signal(barrier, inc=1, device_id=(mate, node), device_id_type=MESH)
-    for other in (up, down, facing):
-        pl.semaphore_signal(barrier, inc=1, device_id=(expert, other), device_id_type=MESH)
+
+    odd_z = (node // 2) % 2
+
+    @pl.when(odd == 0)
+    def _():
+        pl.semaphore_signal(barrier, inc=1, device_id=(expert, facing), device_id_type=MESH)
+
+    @pl.when(odd_z == 0)
+    def _():
+        for other in (up, down):
+            pl.semaphore_signal(barrier, inc=1, device_id=(expert, other), device_id_type=MESH)
 
     def fixed(index):
         return pl.ds(index * cap, cap)
@@ -251,7 +260,17 @@
     for copy in (loads[2], loads[3], load_w, load_m):
         copy.start()
     choose(0, 2, target)
-    pl.semaphore_wait(barrier, 6)
+    pl.semaphore_wait(barrier, 3 + odd + 2 * odd_z)
+
+    @pl.when(odd_z == 1)
+    def _():
+        for other in (up, down):
+            pl.semaphore_signal(ready.at[0], inc=1, device_id=(expert, other), device_id_type=MESH)
+
+    @pl.when(odd == 1)
+    def _():
+        pl.semaphore_signal(ready.at[1], inc=1, device_id=(expert, facing), device_id_type=MESH)
+
     dispatch_copy(0, 2).start()
     for k in (3, 1):
         choose(0, k, target)
@@ -278,8 +297,18 @@
     dispatch_copy(0, 3).wait_recv()
     slopes(0, 1)
     update_moment(0)
+
+    @pl.when(odd_z == 0)
+    def _():
+        pl.semaphore_wait(ready.at[0], 2)
+
     orthogonalize_and_share(0)
     backward(0)
+
+    @pl.when(odd == 0)
+    def _():
+        pl.semaphore_wait(ready.at[1], 1)
+
     pass_across(0)
     start_return(0)
 
@@ -384,6 +413,7 @@
             dma((rounds, 2, PIECES)),
             dma((rounds, PIECES)),
             dma((rounds, PIECES)),
+            pltpu.SemaphoreType.REGULAR((2,)),
         ],
         compiler_params=pltpu.CompilerParams(
             collective_id=0, has_side_effects=True, vmem_limit_bytes=40 << 20

time: 118 us -> 117 us (level)
  Pallas kernels: 118 us -> 116 us
    pallas_call x1, Pallas kernels: 115 us -> 114 us  [on_device(): pl.pallas_call(functools.partial(kernel, nodes), name='muon_rounds', out_...]
where the time goes in v4:
time: 117 us
  Pallas kernels  116 us (99%)
    pallas_call x1, Pallas kernels, on_device(): pl.pallas_call(functools.partial(kernel, nodes), name='muon_rounds', out_...  114 us
    pallas_call x1, Pallas kernels, on_device(): pl.pallas_call(store, name='store_results', out_shape=(jax.ShapeDtypeStru...  2.38 us

profile of v4, /device:TPU:1, one launch (start us, length us, event | category | flops | bytes accessed | tf_op | source)
XLA Modules:
  0.0 116.9 jit_solution(14409683351632944387)
XLA Ops:
  0.6 113.9 %muon_rounds.1 = (f32[1024,512]{1,0:T(8,128)S(1)}, f32[1024,512]{1,0:T(8,128)S(1)}, bf16[2,256,1024]{2,1,0:T(8,128)(2,1)S(1)}) custom-call(bf16[2,256,1024]{2,1,0:T(8,128)(2,1)} %tok_hbm.1, s32[2,256]{1,0:T(2,128)} %route_hbm.1, bf16[2,256,512]{2,1,0:T(8,128)(2,1)} %og_hbm.1, f32[1,1,1024,512]{3,2,1,0:T(8,128)} %w_hbm.1, f32[1,1,1024,512]{3,2,1,0:T(8,128)} %m_hbm.1), custom_call_target="tpu_custom_call" | custom-call | tf_op jit(solution)/shard_map/muon_rounds/pallas_call | solution.py:379
  114.5 2.4 %store_results.1 = (f32[1,1,1024,512]{3,2,1,0:T(8,128)}, f32[1,1,1024,512]{3,2,1,0:T(8,128)}, bf16[2,256,1024]{2,1,0:T(8,128)(2,1)}) custom-call(f32[1024,512]{1,0:T(8,128)S(1)} %get-tuple-element.6.weight, f32[1024,512]{1,0:T(8,128)S(1)} %get-tuple-element.7.moment, bf16[2,256,1024]{2,1,0:T(8,128)(2,1)S(1)} %get-tuple-element.8.ig), custom_call_target="tpu_custom_call" | custom-call | tf_op jit(solution)/shard_map/store_results/pallas_call | solution.py:422

commit v5 on v4

--- a/solution.py
+++ b/solution.py
@@ -113,12 +113,13 @@
             device_id_type=MESH,
         )
 
-    def return_copy(r, k):
+    def return_copy(r, k, part):
+        some = pl.ds(k * cap + part * (cap // 2), cap // 2)
         return pltpu.make_async_remote_copy(
-            src_ref=back.at[r, fixed(k)],
-            dst_ref=ret.at[r, fixed(k)],
-            send_sem=r_send.at[r, k],
-            recv_sem=r_recv.at[r, k],
+            src_ref=back.at[r, some],
+            dst_ref=ret.at[r, some],
+            send_sem=r_send.at[r, k, part],
+            recv_sem=r_recv.at[r, k, part],
             device_id=(mates[k], node),
             device_id_type=MESH,
         )
@@ -143,9 +144,9 @@
             device_id_type=MESH,
         )
 
-    def start_return(r):
-        for k in (2, 3, 1):
-            return_copy(r, k).start()
+    def start_return(r, k):
+        for part in range(2):
+            return_copy(r, k, part).start()
 
     def slopes(r, half):
         part = pl.ds(half * rows, rows)
@@ -210,31 +211,36 @@
 
         lax.fori_loop(0, CHUNKS, last, 0)
 
-    def backward(r):
-        for half in (1, 0):
-            part = pl.ds(half * rows, rows)
-
-            def body(j, carry, part=part):
-                columns = pl.ds(pl.multiple_of(j * tile, tile), tile)
-                grad = dot(slope[part, :], wide[strip(j), :], 1, 1) * factor
-                back[r, part, columns] = grad.astype(BF16)
-                return carry
-
-            lax.fori_loop(0, CHUNKS, body, 0)
-        ret[r, fixed(0), :] = back[r, fixed(0), :]
-
-    def unsort(r):
-        for k in (1, 2, 3):
-            return_copy(r, k).wait_recv()
+    def backward(r, k, blocks):
+        part = pl.ds(k * cap, blocks * cap)
 
         def body(j, carry):
             columns = pl.ds(pl.multiple_of(j * tile, tile), tile)
-            ig[r, :, columns] = dot(table[r], ret[r, :, columns], 0, 0).astype(BF16)
+            grad = dot(slope[part, :], wide[strip(j), :], 1, 1) * factor
+            back[r, part, columns] = grad.astype(BF16)
             return carry
 
         lax.fori_loop(0, CHUNKS, body, 0)
-
-    def pass_across(r):
+        if k == 0:
+            ret[r, fixed(0), :] = back[r, fixed(0), :]
+
+    def unsort(r, k, blocks):
+        for i in range(max(k, 1), k + blocks):
+            return_copy(r, i, 0).wait_recv()
+            return_copy(r, i, 1).wait_recv()
+        part = pl.ds(k * cap, blocks * cap)
+
+        def body(j, carry):
+            columns = pl.ds(pl.multiple_of(j * tile, tile), tile)
+            placed = dot(table[r, part, :], ret[r, part, columns], 0, 0)
+            if k:
+                placed = placed + ig[r, :, columns].astype(F32)
+            ig[r, :, columns] = placed.astype(BF16)
+            return carry
+
+        lax.fori_loop(0, CHUNKS, body, 0)
+
+    def pass_across(r, first, last):
         def body(j, carry):
             z_copy(r, 1 - odd, j).wait_recv()
             own = shared[r, bit(j), :].astype(F32)
@@ -242,7 +248,7 @@
             x_copy(r, j).start()
             return carry
 
-        lax.fori_loop(0, PIECES, body, 0)
+        lax.fori_loop(first, last, body, 0)
 
     def averaged(r, j):
         z_copy(r, odd, j).wait_recv()
@@ -303,14 +309,16 @@
         pl.semaphore_wait(ready.at[0], 2)
 
     orthogonalize_and_share(0)
-    backward(0)
+    backward(0, 2, 2)
+    backward(0, 0, 2)
 
     @pl.when(odd == 0)
     def _():
         pl.semaphore_wait(ready.at[1], 1)
 
-    pass_across(0)
-    start_return(0)
+    pass_across(0, 0, PIECES)
+    for k in (2, 3, 1):
+        start_return(0, k)
 
     def mixed(j, carry):
         wide[bit(j), :] = averaged(0, j).astype(BF16)
@@ -322,24 +330,32 @@
         dispatch_copy(1, k).wait_recv()
     slopes(1, 0)
     slopes(1, 1)
-    backward(1)
-    start_return(1)
+    backward(1, 2, 1)
+    start_return(1, 2)
     update_moment(1)
     orthogonalize_and_share(1)
-    unsort(0)
-    pass_across(1)
-    unsort(1)
+    backward(1, 3, 1)
+    backward(1, 0, 2)
+    start_return(1, 1)
+    pass_across(1, 0, PIECES // 2)
+    return_copy(1, 3, 0).start()
+    unsort(0, 0, 4)
+    pass_across(1, PIECES // 2, PIECES)
+    return_copy(1, 3, 1).start()
+    unsort(1, 0, 3)
 
     def finished(j, carry):
         averaged(1, j)
         return carry
 
     lax.fori_loop(0, PIECES, finished, 0)
+    unsort(1, 3, 1)
 
     for r in range(ROUNDS):
         for k in (1, 2, 3):
             dispatch_copy(r, k).wait_send()
-            return_copy(r, k).wait_send()
+            return_copy(r, k, 0).wait_send()
+            return_copy(r, k, 1).wait_send()
 
         def sent_all(j, carry, r=r):
             z_copy(r, 0, j).wait_send()
@@ -407,8 +423,8 @@
             dma((7,)),
             dma((rounds, 4)),
             dma((rounds, 4)),
-            dma((rounds, 4)),
-            dma((rounds, 4)),
+            dma((rounds, 4, 2)),
+            dma((rounds, 4, 2)),
             dma((rounds, 2, PIECES)),
             dma((rounds, 2, PIECES)),
             dma((rounds, PIECES)),

time: 117 us -> 116 us (level)
    pallas_call x1, Pallas kernels: 114 us -> 112 us  [on_device(): pl.pallas_call(functools.partial(kernel, nodes), name='muon_rounds', out_...]
where the time goes in v5:
time: 116 us; the launch traced here: 115 us
  Pallas kernels  115 us (99%)
    pallas_call x1, Pallas kernels, on_device(): pl.pallas_call(functools.partial(kernel, nodes), name='muon_rounds', out_...  112 us
    pallas_call x1, Pallas kernels, on_device(): pl.pallas_call(store, name='store_results', out_shape=(jax.ShapeDtypeStru...  2.38 us

profile of v5, /device:TPU:1, one launch (start us, length us, event | category | flops | bytes accessed | tf_op | source)
XLA Modules:
  0.0 115.5 jit_solution(12083257820082967627)
XLA Ops:
  0.6 112.4 %muon_rounds.1 = (f32[1024,512]{1,0:T(8,128)S(1)}, f32[1024,512]{1,0:T(8,128)S(1)}, bf16[2,256,1024]{2,1,0:T(8,128)(2,1)S(1)}) custom-call(bf16[2,256,1024]{2,1,0:T(8,128)(2,1)} %tok_hbm.1, s32[2,256]{1,0:T(2,128)} %route_hbm.1, bf16[2,256,512]{2,1,0:T(8,128)(2,1)} %og_hbm.1, f32[1,1,1024,512]{3,2,1,0:T(8,128)} %w_hbm.1, f32[1,1,1024,512]{3,2,1,0:T(8,128)} %m_hbm.1), custom_call_target="tpu_custom_call" | custom-call | tf_op jit(solution)/shard_map/muon_rounds/pallas_call | solution.py:395
  113.1 2.4 %store_results.1 = (f32[1,1,1024,512]{3,2,1,0:T(8,128)}, f32[1,1,1024,512]{3,2,1,0:T(8,128)}, bf16[2,256,1024]{2,1,0:T(8,128)(2,1)}) custom-call(f32[1024,512]{1,0:T(8,128)S(1)} %get-tuple-element.6.weight, f32[1024,512]{1,0:T(8,128)S(1)} %get-tuple-element.7.moment, bf16[2,256,1024]{2,1,0:T(8,128)(2,1)S(1)} %get-tuple-element.8.ig), custom_call_target="tpu_custom_call" | custom-call | tf_op jit(solution)/shard_map/store_results/pallas_call | solution.py:438

commit v6 on v5

--- a/solution.py
+++ b/solution.py
@@ -155,22 +155,18 @@
         slope[part, :] = (grads * 2.0 * jnp.maximum(pre, 0.0)).astype(BF16)
 
     def update_moment(r):
-        def body(j, total):
-            columns = pl.ds(pl.multiple_of(j * tile, tile), tile)
-            grad = dot(got[r, :, columns], slope[...], 0, 0) * factor
-            new = 0.9 * moment[strip(j), :] + grad
-            moment[strip(j), :] = new
-            return total + jnp.sum(new * new, axis=0, keepdims=True)
-
-        total = lax.fori_loop(0, CHUNKS, body, jnp.zeros((1, hidden), F32))
+        total = jnp.zeros((1, hidden), F32)
+        for j in range(CHUNKS):
+            rung = pl.ds(j * tile, tile)
+            grad = dot(got[r, :, rung], slope[...], 0, 0) * factor
+            new = 0.9 * moment[rung, :] + grad
+            moment[rung, :] = new
+            total = total + jnp.sum(new * new, axis=0, keepdims=True)
         norm = jnp.sqrt(jnp.sum(total, axis=1, keepdims=True))
         scale = 1.0 / (norm + 1e-07)
-
-        def scaled(j, carry):
-            orthog[strip(j), :] = (moment[strip(j), :] * scale).astype(BF16)
-            return carry
-
-        lax.fori_loop(0, CHUNKS, scaled, 0)
+        for j in range(CHUNKS):
+            rung = pl.ds(j * tile, tile)
+            orthog[rung, :] = (moment[rung, :] * scale).astype(BF16)
 
     def polynomial():
         part = hidden // 2
@@ -184,43 +180,33 @@
             poly[columns, :] = (-4.775 * own.astype(F32) + 2.0315 * square).astype(BF16)
 
     def applied(j):
-        own = orthog[strip(j), :]
+        own = orthog[pl.ds(j * tile, tile), :]
         return (3.4445 * own.astype(F32) + dot(own, poly[...])).astype(BF16)
 
     def orthogonalize_and_share(r):
         def sweep(i, carry):
             polynomial()
-
-            def body(j, inner):
-                orthog[strip(j), :] = applied(j)
-                return inner
-
-            return lax.fori_loop(0, CHUNKS, body, carry)
+            for j in range(CHUNKS):
+                orthog[pl.ds(j * tile, tile), :] = applied(j)
+            return carry
 
         lax.fori_loop(0, NS_STEPS - 1, sweep, 0)
         polynomial()
-
-        def last(j, carry):
-            stepped = weight[strip(j), :] - step_size * applied(j).astype(F32)
-            weight[strip(j), :] = stepped
-            shared[r, strip(j), :] = stepped.astype(BF16)
+        for j in range(CHUNKS):
+            rung = pl.ds(j * tile, tile)
+            stepped = weight[rung, :] - step_size * applied(j).astype(F32)
+            weight[rung, :] = stepped
+            shared[r, rung, :] = stepped.astype(BF16)
             for i in range(PIECES // CHUNKS):
                 z_copy(r, 0, j * (PIECES // CHUNKS) + i).start()
                 z_copy(r, 1, j * (PIECES // CHUNKS) + i).start()
-            return carry
-
-        lax.fori_loop(0, CHUNKS, last, 0)
 
     def backward(r, k, blocks):
         part = pl.ds(k * cap, blocks * cap)
-
-        def body(j, carry):
-            columns = pl.ds(pl.multiple_of(j * tile, tile), tile)
-            grad = dot(slope[part, :], wide[strip(j), :], 1, 1) * factor
-            back[r, part, columns] = grad.astype(BF16)
-            return carry
-
-        lax.fori_loop(0, CHUNKS, body, 0)
+        for j in range(CHUNKS):
+            rung = pl.ds(j * tile, tile)
+            grad = dot(slope[part, :], wide[rung, :], 1, 1) * factor
+            back[r, part, rung] = grad.astype(BF16)
         if k == 0:
             ret[r, fixed(0), :] = back[r, fixed(0), :]
 
@@ -230,15 +216,12 @@
             return_copy(r, i, 1).wait_recv()
         part = pl.ds(k * cap, blocks * cap)
 
-        def body(j, carry):
-            columns = pl.ds(pl.multiple_of(j * tile, tile), tile)
+        for j in range(CHUNKS):
+            columns = pl.ds(j * tile, tile)
             placed = dot(table[r, part, :], ret[r, part, columns], 0, 0)
             if k:
                 placed = placed + ig[r, :, columns].astype(F32)
             ig[r, :, columns] = placed.astype(BF16)
-            return carry
-
-        lax.fori_loop(0, CHUNKS, body, 0)
 
     def pass_across(r, first, last):
         def body(j, carry):
@@ -330,15 +313,14 @@
         dispatch_copy(1, k).wait_recv()
     slopes(1, 0)
     slopes(1, 1)
-    backward(1, 2, 1)
+    backward(1, 2, 2)
     start_return(1, 2)
+    return_copy(1, 3, 0).start()
     update_moment(1)
     orthogonalize_and_share(1)
-    backward(1, 3, 1)
     backward(1, 0, 2)
     start_return(1, 1)
     pass_across(1, 0, PIECES // 2)
-    return_copy(1, 3, 0).start()
     unsort(0, 0, 4)
     pass_across(1, PIECES // 2, PIECES)
     return_copy(1, 3, 1).start()

time: 116 us -> 113 us (0.974)
  Pallas kernels: 115 us -> 112 us
    pallas_call x1, Pallas kernels: 112 us -> 110 us  [on_device(): pl.pallas_call(functools.partial(kernel, nodes), name='muon_rounds', out_...]
where the time goes in v6:
time: 113 us
  Pallas kernels  112 us (99%)
    pallas_call x1, Pallas kernels, on_device(): pl.pallas_call(functools.partial(kernel, nodes), name='muon_rounds', out_...  110 us
    pallas_call x1, Pallas kernels, on_device(): pl.pallas_call(store, name='store_results', out_shape=(jax.ShapeDtypeStru...  2.38 us

profile of v6, /device:TPU:1, one launch (start us, length us, event | category | flops | bytes accessed | tf_op | source)
XLA Modules:
  0.0 112.8 jit_solution(12430816838167153567)
XLA Ops:
  0.6 109.6 %muon_rounds.1 = (f32[1024,512]{1,0:T(8,128)S(1)}, f32[1024,512]{1,0:T(8,128)S(1)}, bf16[2,256,1024]{2,1,0:T(8,128)(2,1)S(1)}) custom-call(bf16[2,256,1024]{2,1,0:T(8,128)(2,1)} %tok_hbm.1, s32[2,256]{1,0:T(2,128)} %route_hbm.1, bf16[2,256,512]{2,1,0:T(8,128)(2,1)} %og_hbm.1, f32[1,1,1024,512]{3,2,1,0:T(8,128)} %w_hbm.1, f32[1,1,1024,512]{3,2,1,0:T(8,128)} %m_hbm.1), custom_call_target="tpu_custom_call" | custom-call | tf_op jit(solution)/shard_map/muon_rounds/pallas_call | solution.py:377
  110.2 2.4 %store_results.1 = (f32[1,1,1024,512]{3,2,1,0:T(8,128)}, f32[1,1,1024,512]{3,2,1,0:T(8,128)}, bf16[2,256,1024]{2,1,0:T(8,128)(2,1)}) custom-call(f32[1024,512]{1,0:T(8,128)S(1)} %get-tuple-element.6.weight, f32[1024,512]{1,0:T(8,128)S(1)} %get-tuple-element.7.moment, bf16[2,256,1024]{2,1,0:T(8,128)(2,1)S(1)} %get-tuple-element.8.ig), custom_call_target="tpu_custom_call" | custom-call | tf_op jit(solution)/shard_map/store_results/pallas_call | solution.py:420

commit v7 on v6

--- a/solution.py
+++ b/solution.py
@@ -11,7 +11,8 @@
 ROUNDS = 2
 NS_STEPS = 3
 CHUNKS = 4
-PIECES = 8
+PIECES = 16
+DEPTH = 8
 MESH = pl.DeviceIdType.MESH
 F32 = jnp.float32
 BF16 = jnp.bfloat16
@@ -65,16 +66,24 @@
     for mate in mates[1:]:
         pl.semaphore_signal(barrier, inc=1, device_id=(mate, node), device_id_type=MESH)
 
-    odd_z = (node // 2) % 2
+    def leads(other):
+        z = (other // 2) % DEPTH
+        return jnp.where((z == 0) | (z == 3), 1, 0)
+
+    led_up = leads(up)
+    led = leads(node)
 
     @pl.when(odd == 0)
     def _():
         pl.semaphore_signal(barrier, inc=1, device_id=(expert, facing), device_id_type=MESH)
 
-    @pl.when(odd_z == 0)
-    def _():
-        for other in (up, down):
-            pl.semaphore_signal(barrier, inc=1, device_id=(expert, other), device_id_type=MESH)
+    @pl.when(led_up == 0)
+    def _():
+        pl.semaphore_signal(barrier, inc=1, device_id=(expert, up), device_id_type=MESH)
+
+    @pl.when(led == 1)
+    def _():
+        pl.semaphore_signal(barrier, inc=1, device_id=(expert, down), device_id_type=MESH)
 
     def fixed(index):
         return pl.ds(index * cap, cap)
@@ -249,12 +258,15 @@
     for copy in (loads[2], loads[3], load_w, load_m):
         copy.start()
     choose(0, 2, target)
-    pl.semaphore_wait(barrier, 3 + odd + 2 * odd_z)
-
-    @pl.when(odd_z == 1)
-    def _():
-        for other in (up, down):
-            pl.semaphore_signal(ready.at[0], inc=1, device_id=(expert, other), device_id_type=MESH)
+    pl.semaphore_wait(barrier, 3 + odd + led_up + (1 - led))
+
+    @pl.when(led_up == 1)
+    def _():
+        pl.semaphore_signal(ready.at[0], inc=1, device_id=(expert, up), device_id_type=MESH)
+
+    @pl.when(led == 0)
+    def _():
+        pl.semaphore_signal(ready.at[2], inc=1, device_id=(expert, down), device_id_type=MESH)
 
     @pl.when(odd == 1)
     def _():
@@ -287,9 +299,13 @@
     slopes(0, 1)
     update_moment(0)
 
-    @pl.when(odd_z == 0)
-    def _():
-        pl.semaphore_wait(ready.at[0], 2)
+    @pl.when(led == 1)
+    def _():
+        pl.semaphore_wait(ready.at[0], 1)
+
+    @pl.when(led_up == 0)
+    def _():
+        pl.semaphore_wait(ready.at[2], 1)
 
     orthogonalize_and_share(0)
     backward(0, 2, 2)
@@ -313,11 +329,12 @@
         dispatch_copy(1, k).wait_recv()
     slopes(1, 0)
     slopes(1, 1)
-    backward(1, 2, 2)
+    backward(1, 2, 1)
     start_return(1, 2)
-    return_copy(1, 3, 0).start()
     update_moment(1)
     orthogonalize_and_share(1)
+    backward(1, 3, 1)
+    return_copy(1, 3, 0).start()
     backward(1, 0, 2)
     start_return(1, 1)
     pass_across(1, 0, PIECES // 2)
@@ -411,7 +428,7 @@
             dma((rounds, 2, PIECES)),
             dma((rounds, PIECES)),
             dma((rounds, PIECES)),
-            pltpu.SemaphoreType.REGULAR((2,)),
+            pltpu.SemaphoreType.REGULAR((3,)),
         ],
         compiler_params=pltpu.CompilerParams(
             collective_id=0, has_side_effects=True, vmem_limit_bytes=40 << 20

time: 113 us -> 113 us (level)
  no operation moved by 1% of the time
where the time goes in v7:
time: 113 us
  Pallas kernels  112 us (99%)
    pallas_call x1, Pallas kernels, on_device(): pl.pallas_call(functools.partial(kernel, nodes), name='muon_rounds', out_...  110 us
    pallas_call x1, Pallas kernels, on_device(): pl.pallas_call(store, name='store_results', out_shape=(jax.ShapeDtypeStru...  2.38 us

profile of v7, /device:TPU:1, one launch (start us, length us, event | category | flops | bytes accessed | tf_op | source)
XLA Modules:
  0.0 112.9 jit_solution(4176276701487580732)
XLA Ops:
  0.6 109.8 %muon_rounds.1 = (f32[1024,512]{1,0:T(8,128)S(1)}, f32[1024,512]{1,0:T(8,128)S(1)}, bf16[2,256,1024]{2,1,0:T(8,128)(2,1)S(1)}) custom-call(bf16[2,256,1024]{2,1,0:T(8,128)(2,1)} %tok_hbm.1, s32[2,256]{1,0:T(2,128)} %route_hbm.1, bf16[2,256,512]{2,1,0:T(8,128)(2,1)} %og_hbm.1, f32[1,1,1024,512]{3,2,1,0:T(8,128)} %w_hbm.1, f32[1,1,1024,512]{3,2,1,0:T(8,128)} %m_hbm.1), custom_call_target="tpu_custom_call" | custom-call | tf_op jit(solution)/shard_map/muon_rounds/pallas_call | solution.py:394
  110.4 2.4 %store_results.1 = (f32[1,1,1024,512]{3,2,1,0:T(8,128)}, f32[1,1,1024,512]{3,2,1,0:T(8,128)}, bf16[2,256,1024]{2,1,0:T(8,128)(2,1)}) custom-call(f32[1024,512]{1,0:T(8,128)S(1)} %get-tuple-element.6.weight, f32[1024,512]{1,0:T(8,128)S(1)} %get-tuple-element.7.moment, bf16[2,256,1024]{2,1,0:T(8,128)(2,1)S(1)} %get-tuple-element.8.ig), custom_call_target="tpu_custom_call" | custom-call | tf_op jit(solution)/shard_map/store_results/pallas_call | solution.py:437

commit v8 on v7

--- a/solution.py
+++ b/solution.py
@@ -11,7 +11,8 @@
 ROUNDS = 2
 NS_STEPS = 3
 CHUNKS = 4
-PIECES = 16
+PIECES = 8
+EARLY = 2
 DEPTH = 8
 MESH = pl.DeviceIdType.MESH
 F32 = jnp.float32
@@ -133,9 +134,9 @@
             device_id_type=MESH,
         )
 
-    def z_copy(r, way, j):
+    def z_copy(r, way, j, held=shared):
         return pltpu.make_async_remote_copy(
-            src_ref=shared.at[r, bit(j)],
+            src_ref=held.at[r, bit(j)],
             dst_ref=beside.at[r, way, bit(j)],
             send_sem=z_send.at[r, way, j],
             recv_sem=z_recv.at[r, way, j],
@@ -143,9 +144,9 @@
             device_id_type=MESH,
         )
 
-    def x_copy(r, j):
+    def x_copy(r, j, held=pair):
         return pltpu.make_async_remote_copy(
-            src_ref=pair.at[r, bit(j)],
+            src_ref=held.at[r, bit(j)],
             dst_ref=across.at[r, bit(j)],
             send_sem=x_send.at[r, j],
             recv_sem=x_recv.at[r, j],
@@ -206,9 +207,12 @@
             stepped = weight[rung, :] - step_size * applied(j).astype(F32)
             weight[rung, :] = stepped
             shared[r, rung, :] = stepped.astype(BF16)
-            for i in range(PIECES // CHUNKS):
-                z_copy(r, 0, j * (PIECES // CHUNKS) + i).start()
-                z_copy(r, 1, j * (PIECES // CHUNKS) + i).start()
+            for i in range(j * (PIECES // CHUNKS), (j + 1) * (PIECES // CHUNKS)):
+                if i < EARLY:
+                    x_copy(r, i, shared).start()
+                else:
+                    z_copy(r, 0, i).start()
+                    z_copy(r, 1, i).start()
 
     def backward(r, k, blocks):
         part = pl.ds(k * cap, blocks * cap)
@@ -242,14 +246,34 @@
 
         lax.fori_loop(first, last, body, 0)
 
+    def pass_along(r):
+        for j in range(EARLY):
+            z_copy(r, 1 - odd, j).start()
+            x_copy(r, j, shared).wait_recv()
+            own = shared[r, bit(j), :].astype(F32)
+            pair[r, bit(j), :] = (own + across[r, bit(j), :].astype(F32)).astype(BF16)
+            z_copy(r, odd, j, pair).start()
+
     def averaged(r, j):
-        z_copy(r, odd, j).wait_recv()
-        x_copy(r, j).wait_recv()
         neighbours = beside[r, 0, bit(j), :].astype(F32) + beside[r, 1, bit(j), :].astype(F32)
         neighbours = neighbours + across[r, bit(j), :].astype(F32)
         new = 0.4 * weight[bit(j), :] + 0.15 * neighbours
         weight[bit(j), :] = new
         return new
+
+    def averages(r, use):
+        for j in range(EARLY):
+            z_copy(r, 0, j).wait_recv()
+            z_copy(r, 1, j).wait_recv()
+            use(j, averaged(r, j))
+
+        def body(j, carry):
+            z_copy(r, odd, j).wait_recv()
+            x_copy(r, j).wait_recv()
+            use(j, averaged(r, j))
+            return carry
+
+        lax.fori_loop(EARLY, PIECES, body, 0)
 
     load_route.wait()
     target = targets(0)
@@ -307,23 +331,22 @@
     def _():
         pl.semaphore_wait(ready.at[2], 1)
 
+    @pl.when(odd == 0)
+    def _():
+        pl.semaphore_wait(ready.at[1], 1)
+
     orthogonalize_and_share(0)
     backward(0, 2, 2)
     backward(0, 0, 2)
-
-    @pl.when(odd == 0)
-    def _():
-        pl.semaphore_wait(ready.at[1], 1)
-
-    pass_across(0, 0, PIECES)
+    pass_across(0, EARLY, PIECES)
     for k in (2, 3, 1):
         start_return(0, k)
-
-    def mixed(j, carry):
-        wide[bit(j), :] = averaged(0, j).astype(BF16)
-        return carry
-
-    lax.fori_loop(0, PIECES, mixed, 0)
+    pass_along(0)
+
+    def narrowed(j, new):
+        wide[bit(j), :] = new.astype(BF16)
+
+    averages(0, narrowed)
 
     for k in (1, 2, 3):
         dispatch_copy(1, k).wait_recv()
@@ -337,17 +360,13 @@
     return_copy(1, 3, 0).start()
     backward(1, 0, 2)
     start_return(1, 1)
-    pass_across(1, 0, PIECES // 2)
+    pass_across(1, EARLY, PIECES // 2)
     unsort(0, 0, 4)
     pass_across(1, PIECES // 2, PIECES)
     return_copy(1, 3, 1).start()
+    pass_along(1)
     unsort(1, 0, 3)
-
-    def finished(j, carry):
-        averaged(1, j)
-        return carry
-
-    lax.fori_loop(0, PIECES, finished, 0)
+    averages(1, lambda j, new: None)
     unsort(1, 3, 1)
 
     for r in range(ROUNDS):

time: 113 us -> 112 us (level)
  no operation moved by 1% of the time
where the time goes in v8:
time: 112 us
  Pallas kernels  111 us (99%)
    pallas_call x1, Pallas kernels, on_device(): pl.pallas_call(functools.partial(kernel, nodes), name='muon_rounds', out_...  109 us
    pallas_call x1, Pallas kernels, on_device(): pl.pallas_call(store, name='store_results', out_shape=(jax.ShapeDtypeStru...  2.38 us

profile of v8, /device:TPU:1, one launch (start us, length us, event | category | flops | bytes accessed | tf_op | source)
XLA Modules:
  0.0 111.9 jit_solution(6793906726049168636)
XLA Ops:
  0.6 108.7 %muon_rounds.1 = (f32[1024,512]{1,0:T(8,128)S(1)}, f32[1024,512]{1,0:T(8,128)S(1)}, bf16[2,256,1024]{2,1,0:T(8,128)(2,1)S(1)}) custom-call(bf16[2,256,1024]{2,1,0:T(8,128)(2,1)} %tok_hbm.1, s32[2,256]{1,0:T(2,128)} %route_hbm.1, bf16[2,256,512]{2,1,0:T(8,128)(2,1)} %og_hbm.1, f32[1,1,1024,512]{3,2,1,0:T(8,128)} %w_hbm.1, f32[1,1,1024,512]{3,2,1,0:T(8,128)} %m_hbm.1), custom_call_target="tpu_custom_call" | custom-call | tf_op jit(solution)/shard_map/muon_rounds/pallas_call | solution.py:413
  109.4 2.4 %store_results.1 = (f32[1,1,1024,512]{3,2,1,0:T(8,128)}, f32[1,1,1024,512]{3,2,1,0:T(8,128)}, bf16[2,256,1024]{2,1,0:T(8,128)(2,1)}) custom-call(f32[1024,512]{1,0:T(8,128)S(1)} %get-tuple-element.6.weight, f32[1024,512]{1,0:T(8,128)S(1)} %get-tuple-element.7.moment, bf16[2,256,1024]{2,1,0:T(8,128)(2,1)S(1)} %get-tuple-element.8.ig), custom_call_target="tpu_custom_call" | custom-call | tf_op jit(solution)/shard_map/store_results/pallas_call | solution.py:456

commit v9 on v8

--- a/solution.py
+++ b/solution.py
@@ -11,8 +11,8 @@
 ROUNDS = 2
 NS_STEPS = 3
 CHUNKS = 4
-PIECES = 8
-EARLY = 2
+PIECES = 4
+EARLY = 1
 DEPTH = 8
 MESH = pl.DeviceIdType.MESH
 F32 = jnp.float32

time: 112 us -> 112 us (level)
  no operation moved by 1% of the time
where the time goes in v9:
time: 112 us; the launch traced here: 111 us
  Pallas kernels  111 us (99%)
    pallas_call x1, Pallas kernels, on_device(): pl.pallas_call(functools.partial(kernel, nodes), name='muon_rounds', out_...  108 us
    pallas_call x1, Pallas kernels, on_device(): pl.pallas_call(store, name='store_results', out_shape=(jax.ShapeDtypeStru...  2.38 us

profile of v9, /device:TPU:1, one launch (start us, length us, event | category | flops | bytes accessed | tf_op | source)
XLA Modules:
  0.0 111.4 jit_solution(13041402490215776167)
XLA Ops:
  0.6 108.2 %muon_rounds.1 = (f32[1024,512]{1,0:T(8,128)S(1)}, f32[1024,512]{1,0:T(8,128)S(1)}, bf16[2,256,1024]{2,1,0:T(8,128)(2,1)S(1)}) custom-call(bf16[2,256,1024]{2,1,0:T(8,128)(2,1)} %tok_hbm.1, s32[2,256]{1,0:T(2,128)} %route_hbm.1, bf16[2,256,512]{2,1,0:T(8,128)(2,1)} %og_hbm.1, f32[1,1,1024,512]{3,2,1,0:T(8,128)} %w_hbm.1, f32[1,1,1024,512]{3,2,1,0:T(8,128)} %m_hbm.1), custom_call_target="tpu_custom_call" | custom-call | tf_op jit(solution)/shard_map/muon_rounds/pallas_call | solution.py:413
  108.9 2.4 %store_results.1 = (f32[1,1,1024,512]{3,2,1,0:T(8,128)}, f32[1,1,1024,512]{3,2,1,0:T(8,128)}, bf16[2,256,1024]{2,1,0:T(8,128)(2,1)}) custom-call(f32[1024,512]{1,0:T(8,128)S(1)} %get-tuple-element.6.weight, f32[1024,512]{1,0:T(8,128)S(1)} %get-tuple-element.7.moment, bf16[2,256,1024]{2,1,0:T(8,128)(2,1)S(1)} %get-tuple-element.8.ig), custom_call_target="tpu_custom_call" | custom-call | tf_op jit(solution)/shard_map/store_results/pallas_call | solution.py:456
